TPU v7x, 256 devices: a whole 4x4x8 slice. The times are simulated.
256 devices in a mesh: seq: 16 (over y, x), exp: 16 (over z, core).
Axes of the slice: x: 4, y: 4, z: 8, core: 2. Of those that a mesh axis runs over, the one named last changes fastest.
Arguments:
- hidden_in: bfloat16 [8192, 2048], P(('seq', 'exp')), may hold values from -6 to 6
- query_proj: bfloat16 [8192, 2048], P('seq', 'exp'), may hold values from -40 to 40
- key_proj: bfloat16 [8192, 2048], P('seq', 'exp'), may hold values from -40 to 40
- value_proj: bfloat16 [8192, 4096], P('seq', 'exp'), may hold values from -6 to 6
- gate_proj: bfloat16 [8192, 4096], P('seq', 'exp'), may hold values from -6 to 6
- log_decay: float32 [32, 8192], P('exp', 'seq'), may hold values from -0.6 to 0
- write_rate: float32 [32, 8192], P('exp', 'seq'), may hold values from 0 to 1
- head_gain: float32 [128], replicated, may hold values from 0.1 to 1.9
- out_weight: bfloat16 [4096, 2048], P('exp'), may hold values from -0.09375 to 0.09375
- post_gain: float32 [2048], replicated, may hold values from 0.1 to 1.9
- expert_ids: int32 [8192, 4], P(('seq', 'exp')), may hold values from 0 to 15, all different within a row; in each aligned block of 32 rows (0 to 31, 32 to 63, ...) at most 16 rows name the same one
- route_weight: bfloat16 [8192, 4], P(('seq', 'exp')), may hold values from 0.19921875 to 1
- gate_weight: bfloat16 [16, 2048, 512], P('exp'), may hold values from -0.125 to 0.125
- up_weight: bfloat16 [16, 2048, 512], P('exp'), may hold values from -0.125 to 0.125
- down_weight: bfloat16 [16, 512, 2048], P('exp'), may hold values from -0.25 to 0.25
Outputs:
- layer_out: bfloat16 [8192, 2048], P(('seq', 'exp'))
Inputs may be any that keep to these rules, and one draw needn't show every extreme that they name: `expert_ids`: each token names 4 different experts. Within the tokens of one device (aligned blocks of 32 tokens in sequence order) no expert is named by more than 16 tokens, and in every draw some block names some expert exactly 16 times.
All inputs are finite; a program needn't handle non-finite values.
Results may differ from a plain program's by a relative error of at most 0.02.
Values may be sent and summed in bfloat16 or wider, within the bound.
A program may use at most 128 MiB of HBM per device.

v0:
```python
import jax
import jax.numpy as jnp
from jax import lax
from jax.sharding import PartitionSpec as P

D = 2048
DK = 128
DV = 128


EPS = 1e-06
HIGHEST_ACCURACY = lax.Precision.HIGHEST


def prefix(array, axis, join, neutral):
    place = lax.axis_index(axis)
    gathered = jax.tree.map(
        lambda a, kind: lax.all_gather(a.astype(kind), axis), array, (jnp.bfloat16, jnp.bfloat16)
    )
    state = jax.tree.map(lambda a, e: jnp.zeros_like(a) + jnp.asarray(e, a.dtype), array, neutral)

    def one(hop, state):
        return join(
            state,
            jax.tree.map(
                lambda a, own: lax.dynamic_index_in_dim(a, hop, 0, False).astype(own.dtype),
                gathered,
                array,
            ),
        )

    return lax.fori_loop(0, place, one, state)


def unit_rows(matrix):
    return matrix * lax.rsqrt(jnp.sum(matrix * matrix, axis=-1, keepdims=True) + EPS)


def compose(preceding_part, following_part):
    return (
        jnp.einsum(
            "hkl,hlm->hkm", following_part[0], preceding_part[0], precision=HIGHEST_ACCURACY
        ),
        jnp.einsum("jbe,jew->jbw", following_part[0], preceding_part[1], precision=HIGHEST_ACCURACY)
        + following_part[1],
    )


def expert_rows(picked, gate_weight, up_weight, down_weight):
    gate_act = jnp.dot(picked, gate_weight[0], preferred_element_type=jnp.float32)
    up_act = jnp.dot(picked, up_weight[0], preferred_element_type=jnp.float32)
    hidden = (jax.nn.silu(gate_act) * up_act).astype(jnp.bfloat16)
    return jnp.dot(hidden, down_weight[0], preferred_element_type=jnp.float32).astype(jnp.bfloat16)


def recurrent_mix(query_proj, key_proj, value_proj, gate_proj, log_decay, write_rate, head_gain):
    length = value_proj.shape[0]
    head_count = value_proj.shape[1] // DV
    key_heads = query_proj.shape[1] // DK
    group_size = head_count // key_heads
    block_len = min(128, length)
    block_count = length // block_len

    def to_blocks(matrix, inner):
        return matrix.reshape(block_count, block_len, head_count, inner).transpose(2, 0, 1, 3)

    query_unit = unit_rows(query_proj.astype(jnp.float32).reshape(length, key_heads, DK)) * DK ** (
        -0.5
    )
    key_unit = unit_rows(key_proj.astype(jnp.float32).reshape(length, key_heads, DK))
    query_blocks = to_blocks(jnp.repeat(query_unit, group_size, axis=1), DK)
    key_blocks = to_blocks(jnp.repeat(key_unit, group_size, axis=1), DK)
    value_blocks = to_blocks(value_proj.astype(jnp.float32).reshape(length, head_count, DV), DV)
    rate_blocks = write_rate.reshape(head_count, block_count, block_len)
    cum_decay = jnp.cumsum(log_decay.reshape(head_count, block_count, block_len), axis=-1)
    token_position = jnp.arange(block_len)
    causal = token_position[:, None] >= token_position[None, :]
    strict = token_position[:, None] > token_position[None, :]
    gap_decay = cum_decay[..., :, None] - cum_decay[..., None, :]
    decay_mask = jnp.where(causal, jnp.exp(jnp.where(causal, gap_decay, 0.0)), 0.0)
    key_rated = key_blocks * rate_blocks[..., None]
    strict_part = (
        jnp.einsum("hnik,hnjk->hnij", key_rated, key_blocks, precision=HIGHEST_ACCURACY)
        * decay_mask
        * strict
    )
    unit_lower = jnp.eye(block_len, dtype=jnp.float32) + strict_part
    right_sides = jnp.concatenate(
        [key_rated * jnp.exp(cum_decay)[..., None], value_blocks * rate_blocks[..., None]], axis=-1
    )
    solved = jax.scipy.linalg.solve_triangular(
        unit_lower, right_sides, lower=True, unit_diagonal=True
    )
    key_carry = solved[..., :DK]
    value_base = solved[..., DK:]
    end_decay = cum_decay[..., -1]
    key_tail = key_blocks * jnp.exp(end_decay[..., None] - cum_decay)[..., None]
    identity_dk = jnp.eye(DK, dtype=jnp.float32)
    step_map = jnp.exp(end_decay)[..., None, None] * identity_dk - jnp.einsum(
        "hnik,hnil->hnkl", key_tail, key_carry, precision=HIGHEST_ACCURACY
    )
    step_bias = jnp.einsum("hnik,hniv->hnkv", key_tail, value_base, precision=HIGHEST_ACCURACY)
    scores = (
        jnp.einsum("hnik,hnjk->hnij", query_blocks, key_blocks, precision=HIGHEST_ACCURACY)
        * decay_mask
    )
    query_scaled = query_blocks * jnp.exp(cum_decay)[..., None]

    def fold_block(running, step_pair):
        running_map, cumulative_bias = running
        block_transform, block_bias = step_pair
        advanced = (
            jnp.einsum("hkl,hlm->hkm", block_transform, running_map, precision=HIGHEST_ACCURACY),
            jnp.einsum("jbe,jew->jbw", block_transform, cumulative_bias, precision=HIGHEST_ACCURACY)
            + block_bias,
        )
        return (advanced, running)

    start_map = jnp.broadcast_to(identity_dk, (head_count, DK, DK))
    start_bias = jnp.zeros((head_count, DK, DV), jnp.float32)
    totals, prefixes = lax.scan(
        fold_block,
        (start_map, start_bias),
        (step_map.transpose(1, 0, 2, 3), step_bias.transpose(1, 0, 2, 3)),
    )
    total_map, total_bias = totals
    prefix_map, prefix_bias = prefixes
    entering = prefix((total_map, total_bias), "seq", compose, (start_map, start_bias))
    start_state = entering[1]
    block_states = (
        jnp.einsum("nhkl,hlv->nhkv", prefix_map, start_state, precision=HIGHEST_ACCURACY)
        + prefix_bias
    ).transpose(1, 0, 2, 3)
    value_new = value_base - jnp.einsum(
        "hnik,hnkv->hniv", key_carry, block_states, precision=HIGHEST_ACCURACY
    )
    readout = jnp.einsum(
        "hnik,hnkv->hniv", query_scaled, block_states, precision=HIGHEST_ACCURACY
    ) + jnp.einsum("hnij,hnjv->hniv", scores, value_new, precision=HIGHEST_ACCURACY)
    readout = readout.transpose(1, 2, 0, 3).reshape(length, head_count, DV)
    gate_heads = gate_proj.astype(jnp.float32).reshape(length, head_count, DV)
    scaled = readout * lax.rsqrt(jnp.mean(readout * readout, axis=-1, keepdims=True) + EPS)
    return (
        (scaled * head_gain * jax.nn.silu(gate_heads))
        .reshape(length, head_count * DV)
        .astype(jnp.bfloat16)
    )


def per_device(
    hidden_in,
    query_proj,
    key_proj,
    value_proj,
    gate_proj,
    log_decay,
    write_rate,
    head_gain,
    out_weight,
    post_gain,
    expert_ids,
    route_weight,
    gate_weight,
    up_weight,
    down_weight,
):
    mixed = recurrent_mix(
        query_proj, key_proj, value_proj, gate_proj, log_decay, write_rate, head_gain
    )
    tok_dev = hidden_in.shape[0]
    picked = mixed
    projected = lax.psum_scatter(
        jnp.dot(picked, out_weight, preferred_element_type=jnp.float32).astype(jnp.bfloat16),
        "exp",
        scatter_dimension=0,
        tiled=True,
    ).astype(jnp.float32)
    residual = hidden_in.astype(jnp.float32) + projected
    normed = (
        residual
        * lax.rsqrt(jnp.mean(residual * residual, axis=-1, keepdims=True) + EPS)
        * post_gain
    ).astype(jnp.bfloat16)
    top_count = expert_ids.shape[1]
    owners = lax.axis_size("exp")
    capacity = tok_dev * top_count * 2 // owners
    row_total = tok_dev * top_count
    flat_ids = expert_ids.reshape(-1)
    one_hot = (flat_ids[:, None] == jnp.arange(owners, dtype=jnp.int32)[None, :]).astype(jnp.int32)
    own_rank = jnp.sum((jnp.cumsum(one_hot, axis=0) - 1) * one_hot, axis=1)
    target = flat_ids * capacity + own_rank
    source_tok = jnp.arange(row_total, dtype=jnp.int32) // top_count
    outgoing = jnp.zeros((owners * capacity, D), jnp.bfloat16).at[target].set(normed[source_tok])
    outgoing = outgoing.reshape(owners, capacity, D)
    incoming = lax.all_to_all(outgoing, "exp", split_axis=0, concat_axis=0, tiled=True)
    in_shape = incoming.shape
    produced = expert_rows(incoming.reshape(-1, D), gate_weight, up_weight, down_weight).reshape(
        in_shape
    )
    returned = lax.all_to_all(produced, "exp", split_axis=0, concat_axis=0, tiled=True)
    picked = returned.reshape(owners * capacity, D)[target]
    weighted = picked.astype(jnp.float32) * route_weight.reshape(-1)[:, None].astype(jnp.float32)
    combined = residual + jnp.sum(weighted.reshape(tok_dev, top_count, D), axis=1)
    return combined.astype(jnp.bfloat16)


def solution(mesh):
    in_specs = (
        P(("seq", "exp"), None),
        P("seq", "exp"),
        P("seq", "exp"),
        P("seq", "exp"),
        P("seq", "exp"),
        P("exp", "seq"),
        P("exp", "seq"),
        P(),
        P("exp", None),
        P(),
        P(("seq", "exp"), None),
        P(("seq", "exp"), None),
        P("exp", None, None),
        P("exp", None, None),
        P("exp", None, None),
    )
    out_specs = P(("seq", "exp"), None)
    return jax.shard_map(
        per_device, mesh=mesh, in_specs=in_specs, out_specs=out_specs, check_vma=False
    )
```

profile of v0, /device:TPU:8, one launch (start us, length us, event | category | flops | bytes accessed | tf_op | source)
XLA Modules:
  0.0 393.5 jit_solution(5044109614096184604)
XLA Ops:
  6.6 0.8 reshape.219
  8.3 1.1 fusion.65
  9.4 1.0 convert_multiply_fusion.1
  10.4 0.7 mul.211
  11.1 1.2 reshape.227
  12.5 2.1 fusion.27
  14.5 80.1 %custom-call.4 = f32[2,4,1,128,128]{3,4,2,1,0:T(8,128)} custom-call(f32[2,4,1,128,128]{4,3,2,1,0:T(8,128)} %fusion.27), custom_call_target="InvertDiagBlocksLowerTriangular" | custom-call | tf_op jit(solution)/shard_map/jit(_solve_triangular)/vmap(vmap())/triangular_solve | solution.py:91
  94.9 0.7 copy-done.6
  95.6 1.0 fusion.34
  96.7 2.0 convolution_bitcast_fusion.1
  98.7 2.0 fusion.28
  100.6 21.8 %while.30 = (s32[]{:T(128)}, f32[2,128,128]{2,1,0:T(8,128)S(1)}, f32[2,128,128]{2,1,0:T(8,128)}, f32[4,2,128,128]{3,2,0,1:T(8,128)}, f32[4,2,128,128]{2,3,0,1:T(...) while((s32[]{:T(128)}, f32[2,128,128]{2,1,0:T(8,128)S(1)}, ...), condition=%wide.region_4.5_spmd.clone, body=%wide.region_3.4_spmd.clone.sunk | while | flops 100761600 | bytes 2493032 | solution.py:121
  100.7 0.9 copy.120
  101.6 1.9 convolution_add_fusion.6
  103.6 0.7 constant_dynamic-update-slice_fusion.2
  104.3 0.7 bitcast_dynamic-update-slice_fusion.2
  104.9 1.2 fusion.113
  106.1 0.9 copy.120
  107.0 1.9 convolution_add_fusion.6
  109.0 0.7 constant_dynamic-update-slice_fusion.2
  109.7 0.7 bitcast_dynamic-update-slice_fusion.2
  110.4 1.2 fusion.113
  111.6 0.9 copy.120
  112.5 1.9 convolution_add_fusion.6
  114.5 0.7 constant_dynamic-update-slice_fusion.2
  115.2 0.7 bitcast_dynamic-update-slice_fusion.2
  115.8 1.2 fusion.113
  117.0 0.9 copy.120
  117.9 1.9 convolution_add_fusion.6
  120.0 0.7 constant_dynamic-update-slice_fusion.2
  120.6 0.7 bitcast_dynamic-update-slice_fusion.2
  121.3 1.2 fusion.113
  122.5 0.6 convert_element_type.91
  123.2 1.5 convert_element_type.92
  124.8 1.1 fusion.63
  125.9 1.0 fusion.64
  126.9 3.0 convolution_multiply_fusion
  129.9 43.6 %all-gather.5.cloned.1.call-done = bf16[32,128,128]{2,1,0:T(8,128)(2,1)} async-done(((bf16[2,128,128]{2,1,0:T(8,128)(2,1)}), bf16[32,128,128]{2,1,0:T(8,128)(2,1)}) %all-gather.5.cloned.1.call-update) | async-done | bytes 1048592 | tf_op jit(solution)/shard_map/all_gather | solution.py:18
  173.4 49.5 %all-gather.7.cloned.1.call-done = bf16[32,128,128]{2,1,0:T(8,128)(2,1)} async-done(((bf16[2,128,128]{2,1,0:T(8,128)(2,1)}), bf16[32,128,128]{2,1,0:T(8,128)(2,1)}) %all-gather.7.cloned.1.call-update) | async-done | bytes 1048592 | tf_op jit(solution)/shard_map/all_gather | solution.py:18
  222.9 4.7 %while.29 = (s32[]{:T(128)}, f32[2,128,128]{2,1,0:T(8,128)S(1)}, s32[]{:T(128)}, bf16[16,2,128,128]{3,2,1,0:T(8,128)(2,1)}, bf16[16,2,128,128]{3,2,1,0:T(8,128)(2,1)}, /*index=5*/s32[]{:T(128)}, s32[]{:T(128)}, s32[]{:T(128)}) while((s32[]{:T(128)}, f32[2,128,128]{2,1,0:T(8,128)S(1)}, s32[]{:T(128)}, bf16[16,2,128,128]{3,2,1,0:T(8,128)(2,1)}, ...), condition=%wide.region_6.7_spmd, body=%wide.region_5.6_spmd.sunk | while | flops 50397188 | bytes 656503 | solution.py:32
  223.0 1.1 convolution_add_fusion.5
  224.1 1.1 convolution_add_fusion.5
  225.3 1.1 convolution_add_fusion.5
  226.4 1.1 convolution_add_fusion.5
  227.7 1.9 fusion.30
  229.6 1.2 convolution_subtract_fusion
  230.8 1.3 fusion.57
  232.1 1.0 multiply_reduce_fusion.1
  234.2 3.5 convolution_convert_fusion
  237.7 0.7 copy-done.9
  239.2 69.5 %reduce-scatter.2.cloned.1.call-done = bf16[32,2048]{1,0:T(8,128)(2,1)} async-done(((bf16[512,2048]{1,0:T(8,128)(2,1)}), bf16[32,2048]{1,0:T(8,128)(2,1)}) %reduce-scatter.2.cloned.1.call-update) | async-done | bytes 131088 | tf_op jit(solution)/shard_map/reduce_scatter | solution.py:172
  308.7 1.1 multiply_reduce_fusion.2
  309.8 1.0 multiply_convert_fusion
  310.8 3.4 scatter_custom_fusion
  314.2 31.3 %all_to_all.10 = bf16[16,16,2048]{2,1,0:T(8,128)(2,1)S(1)} all-to-all(bf16[16,16,2048]{2,1,0:T(8,128)(2,1)S(1)} %bitcast.138), channel_id=1, replica_groups=mesh['seq'=16,'exp'=16] {'exp'}, dimensions={0} | all-to-all | bytes 2097152 | tf_op jit(solution)/shard_map/all_to_all | solution.py:195
  345.4 1.0 copy-done.5
  346.4 0.7 fusion.17
  347.2 4.3 %convolution_convert_fusion.1 = bf16[256,2048]{1,0:T(8,128)(2,1)} fusion(bf16[1,512,2048]{2,1,0:T(8,128)(2,1)S(1)} %copy-done, bf16[256,2048]{1,0:T(8,128)(2,1)} %bitcast.144, bf16[1,2048,512]{2,1,0:T(8,128)(2,1)} %param.32, f32[256,512]{1,0:T(8,128)S(1)} %fusion.17), kind=kOutput, calls=%fused_computation.23 | convolution fusion | flops 1075052544 | bytes 6815744 | tf_op jit(solution)/shard_map/dot_general | solution.py:53
  351.5 4.3 %all-to-all-start.1 = ((bf16[16,16,2048]{2,1,0:T(8,128)(2,1)}), bf16[16,16,2048]{2,1,0:T(8,128)(2,1)S(1)}, u32[]{:S(2)}, u32[]{:S(2)}) async-start(bf16[16,16,2048]{2,1,0:T(8,128)(2,1)} %bitcast.142), calls=%async_computation.2 | async-start | bytes 2097152 | tf_op jit(solution)/shard_map/all_to_all | solution.py:200
  355.9 26.5 %all-to-all-done.1 = bf16[16,16,2048]{2,1,0:T(8,128)(2,1)S(1)} async-done(((bf16[16,16,2048]{2,1,0:T(8,128)(2,1)}), bf16[16,16,2048]{2,1,0:T(8,128)(2,1)S(1)}, u32[]{:S(2)}, u32[]{:S(2)}) %all-to-all-start.1) | async-done | bytes 1048608 | tf_op jit(solution)/shard_map/all_to_all | solution.py:200
  382.4 1.7 gather_fusion
  384.1 1.4 reshape.226
  385.6 0.7 multiply_reduce_fusion
  386.3 0.7 add_convert_fusion
  (80 shorter events, 4.0 us)
Async XLA Ops:
  6.5 340.6 %copy-start = (bf16[1,512,2048]{2,1,0:T(8,128)(2,1)S(1)}, bf16[1,512,2048]{2,1,0:T(8,128)(2,1)}, u32[]{:S(2)}) copy-start(bf16[1,512,2048]{2,1,0:T(8,128)(2,1)} %param.33) | copy-start | bytes 6291460
  6.5 166.9 %all-gather.5.cloned.1.call-start = ((), (), s32[]{:S(2)}) async-start(), calls=%async_computation.4 | async-start | bytes 1114112 | tf_op jit(solution)/shard_map/all_gather | solution.py:18
  10.4 88.2 %copy-start.1 = (f32[512,128]{1,0:T(8,128)}, f32[512,128]{1,0:T(8,128)S(1)}, u32[]{:S(2)}) copy-start(f32[512,128]{1,0:T(8,128)S(1)} %convert_multiply_fusion.1) | copy-start | bytes 786436
  12.4 84.2 %copy-start.7 = (pred[128,128]{1,0:T(8,128)(4,1)}, pred[128,128]{1,0:T(8,128)(4,1)S(1)}, u32[]{:S(2)}) copy-start(pred[128,128]{1,0:T(8,128)(4,1)S(1)} %get-tuple-element.169) | copy-start | bytes 49156
  94.6 1.0 copy-start.6
  100.6 25.2 %copy-start.12 = (f32[128]{0:T(128)S(1)}, f32[128]{0:T(128)}, u32[]{:S(2)}) copy-start(f32[128]{0:T(128)} %param.26) | copy-start | bytes 1540
  123.1 99.8 %all-gather.7.cloned.1.call-start = ((), (), s32[]{:S(2)}) async-start(), calls=%async_computation.5 | async-start | bytes 1114112 | tf_op jit(solution)/shard_map/all_gather | solution.py:18
  124.7 184.0 %reduce-scatter.2.cloned.1.call-start = ((), (), s32[]{:S(2)}) async-start(), calls=%async_computation.3 | async-start | bytes 2228224 | tf_op jit(solution)/shard_map/reduce_scatter | solution.py:172
  227.7 4.4 %copy-start.2 = (f32[2,4,128,128]{3,2,1,0:T(8,128)S(1)}, f32[2,4,128,128]{3,2,1,0:T(8,128)}, u32[]{:S(2)}) copy-start(f32[2,4,128,128]{3,2,1,0:T(8,128)} %convolution_multiply_fusion) | copy-start | bytes 1572868
  237.6 0.7 copy-start.9
  237.6 71.1 %copy-start.3 = (bf16[32,2048]{1,0:T(8,128)(2,1)S(1)}, bf16[32,2048]{1,0:T(8,128)(2,1)}, u32[]{:S(2)}) copy-start(bf16[32,2048]{1,0:T(8,128)(2,1)} %param.19) | copy-start | bytes 393220
  237.6 72.1 %copy-start.8 = (f32[2048]{0:T(1024)S(1)}, f32[2048]{0:T(1024)}, u32[]{:S(2)}) copy-start(f32[2048]{0:T(1024)} %param.28) | copy-start | bytes 24580
  314.2 32.3 %copy-start.11 = (bf16[1,2048,512]{2,1,0:T(8,128)(2,1)S(1)}, bf16[1,2048,512]{2,1,0:T(8,128)(2,1)}, u32[]{:S(2)}) copy-start(bf16[1,2048,512]{2,1,0:T(8,128)(2,1)} %param.31) | copy-start | bytes 6291460
  345.4 1.0 copy-start.5
  351.4 4.3 %copy-start.10 = (bf16[32,4]{0,1:T(4,128)(2,1)S(1)}, bf16[32,4]{0,1:T(4,128)(2,1)}, u32[]{:S(2)}) copy-start(bf16[32,4]{0,1:T(4,128)(2,1)} %param.30) | copy-start | bytes 772
  351.5 31.0 %all-to-all-start.1 = ((bf16[16,16,2048]{2,1,0:T(8,128)(2,1)}), bf16[16,16,2048]{2,1,0:T(8,128)(2,1)S(1)}, u32[]{:S(2)}, u32[]{:S(2)}) async-start(bf16[16,16,2048]{2,1,0:T(8,128)(2,1)} %bitcast.142), calls=%async_computation.2 | async-start | bytes 2097152 | tf_op jit(solution)/shard_map/all_to_all | solution.py:200
  384.1 2.2 copy-start.4
Sparse Core Ops, SparseCore 0:
  123.3 50.1 all-gather.4
  175.9 47.0 all-gather.6
  237.8 70.8 reduce-scatter.1
where the time goes:
time: 398 us; the launch traced here: 394 us
  waiting for transfers between devices  189 us (47%)
  other arithmetic  91.6 us (23%)
  matrix products  40.5 us (10%)
  blocking collectives  31.3 us (8%)
  local copies, waits for them, and re-layouts  22.7 us (6%)
  between operations  13.5 us (3%)
  starting transfers between devices  4.41 us (1%)
    all_gather x2, waiting for transfers between devices, prefix(): lax.all_gather(a.astype(kind), axis)  93 us
    another operation x3, other arithmetic, recurrent_mix(): jax.scipy.linalg.solve_triangular(unit_lower, right_sides, lower=True, un...  80.1 us
    reduce_scatter x1, waiting for transfers between devices, per_device(): lax.psum_scatter(jnp.dot(picked, out_weight, preferred_element_type=jnp.f...  69.5 us
    all_to_all x1, blocking collectives, per_device(): lax.all_to_all(outgoing, 'exp', split_axis=0, concat_axis=0, tiled=True)  31.3 us
    all_to_all x1, waiting for transfers between devices, per_device(): lax.all_to_all(produced, 'exp', split_axis=0, concat_axis=0, tiled=True)  26.5 us
  transfers between devices with their start and end apart: 4, of which 4 were waited for; matrix products, arithmetic and copies ran while one was open for 2% of the time, Pallas kernels for 0%

commit v1 on v0

v1 whole, which is shorter than its diff:
```python
import functools

import jax
import jax.numpy as jnp
from jax import lax
from jax.experimental import pallas as pl
from jax.experimental.pallas import tpu as pltpu
from jax.sharding import PartitionSpec as P

D = 2048
FF = 512
DK = 128
DV = 128
EPS = 1e-06
CH = 128
HALF = D // 2
F32 = jnp.float32
BF16 = jnp.bfloat16
MESH = pl.DeviceIdType.MESH
NN = (((1,), (0,)), ((), ()))
NT = (((1,), (1,)), ((), ()))
TN = (((0,), (0,)), ((), ()))


def mm(a, b, dims=NN):
    return lax.dot_general(a, b, dims, preferred_element_type=F32)


def split(a):
    hi = a.astype(BF16)
    return hi, (a - hi.astype(F32)).astype(BF16)


def mm3(a, b, dims=NN):
    ah, al = a if isinstance(a, tuple) else split(a)
    bh, bl = b if isinstance(b, tuple) else split(b)
    return mm(ah, bh, dims) + (mm(ah, bl, dims) + mm(al, bh, dims))


def mm2(a, b, dims=NN):
    bh, bl = split(b)
    return mm(a, bh, dims) + mm(a, bl, dims)


def greet(axis, peers):
    barrier = pltpu.get_barrier_semaphore()
    for peer in peers:
        pl.semaphore_signal(barrier, inc=1, device_id={axis: peer}, device_id_type=MESH)
    pl.semaphore_wait(barrier, len(peers))


def send_to(src, dst, send_sem, recv_sem, axis, peer):
    return pltpu.make_async_remote_copy(
        src_ref=src,
        dst_ref=dst,
        send_sem=send_sem,
        recv_sem=recv_sem,
        device_id={axis: peer},
        device_id_type=MESH,
    )


class Gather4:
    def __init__(self, slots, me, right, left, ssem, rsem):
        before, after = lax.rem(me + 3, 4), lax.rem(me + 1, 4)
        self.own = [
            send_to(slots.at[me], slots.at[me], ssem.at[0], rsem.at[0], "seq", right),
            send_to(slots.at[me], slots.at[me], ssem.at[1], rsem.at[1], "seq", left),
        ]
        self.arrive = [
            send_to(slots.at[before], slots.at[before], ssem.at[0], rsem.at[0], "seq", right),
            send_to(slots.at[after], slots.at[after], ssem.at[1], rsem.at[1], "seq", left),
        ]
        self.onward = [
            send_to(
                slots.at[before, 0], slots.at[before, 0], ssem.at[2], rsem.at[2], "seq", right
            ),
            send_to(slots.at[after, 1], slots.at[after, 1], ssem.at[3], rsem.at[3], "seq", left),
        ]
        far = lax.rem(me + 2, 4)
        self.far = [
            send_to(slots.at[far, 0], slots.at[far, 0], ssem.at[2], rsem.at[2], "seq", right),
            send_to(slots.at[far, 1], slots.at[far, 1], ssem.at[3], rsem.at[3], "seq", left),
        ]

    def start(self):
        for copy in self.own:
            copy.start()

    def forward(self):
        for came, on in zip(self.arrive, self.onward):
            came.wait_recv()
            on.start()

    def finish(self):
        for copy in self.far:
            copy.wait_recv()

    def drain(self):
        for copy in self.own + self.onward:
            copy.wait_send()


def compose(later, earlier):
    later = later.astype(F32)
    earlier = earlier.astype(F32)
    joined = mm3(later[:, :DK], earlier)
    return joined + jnp.concatenate([jnp.zeros((DK, DK), F32), later[:, DK:]], axis=1)


def seq_kernel(
    q_ref,
    k_ref,
    v_ref,
    g_ref,
    ld_ref,
    wr_ref,
    gain_ref,
    o_ref,
    xs,
    ys,
    xsend,
    xrecv,
    ysend,
    yrecv,
):
    place = lax.axis_index("seq")
    x, y = lax.rem(place, 4), lax.div(place, 4)
    x_right, x_left = y * 4 + lax.rem(x + 1, 4), y * 4 + lax.rem(x + 3, 4)
    y_right, y_left = lax.rem(y + 1, 4) * 4 + x, lax.rem(y + 3, 4) * 4 + x
    greet("seq", (x_right, x_left, y_right, y_left))

    chunks = q_ref.shape[0] // CH
    row = lax.broadcasted_iota(jnp.int32, (CH, CH), 0)
    col = lax.broadcasted_iota(jnp.int32, (CH, CH), 1)
    eye = row == col
    causal = row >= col
    strict = row > col
    pairs = [(n, h) for n in range(chunks) for h in range(2)]

    keys, kk, qk, queries = [], [], [], []
    for n in range(chunks):
        rows = slice(n * CH, (n + 1) * CH)
        k = k_ref[rows, :].astype(F32)
        k = k * lax.rsqrt(jnp.sum(k * k, axis=-1, keepdims=True) + EPS)
        q = q_ref[rows, :].astype(F32)
        q = q * lax.rsqrt(jnp.sum(q * q, axis=-1, keepdims=True) + EPS) * DK ** (-0.5)
        ks = split(k)
        keys.append(k)
        queries.append(q)
        kk.append(mm3(ks, ks, NT))
        qk.append(mm3(split(q), ks, NT))

    decay, grow, tail, end, strict_part, rate = {}, {}, {}, {}, {}, {}
    for n, h in pairs:
        ld_row = ld_ref[h : h + 1, n * CH : (n + 1) * CH]
        ld_all = jnp.broadcast_to(ld_row, (CH, CH))
        wr_all = jnp.broadcast_to(wr_ref[h : h + 1, n * CH : (n + 1) * CH], (CH, CH))
        ld_col = jnp.sum(jnp.where(eye, ld_all, 0.0), axis=1, keepdims=True)
        cum_col = jnp.sum(jnp.where(causal, ld_all, 0.0), axis=1, keepdims=True)
        cum_row = jnp.sum(jnp.where(row <= col, ld_col, 0.0), axis=0, keepdims=True)
        rate[n, h] = jnp.sum(jnp.where(eye, wr_all, 0.0), axis=1, keepdims=True)
        total = jnp.sum(ld_row, axis=1, keepdims=True)
        decay[n, h] = jnp.where(causal, jnp.exp(jnp.where(causal, cum_col - cum_row, 0.0)), 0.0)
        grow[n, h] = jnp.exp(cum_col)
        tail[n, h] = jnp.exp(total - cum_col)
        end[n, h] = jnp.exp(total)
        strict_part[n, h] = jnp.where(strict, kk[n] * decay[n, h] * rate[n, h], 0.0)

    inverse = {}
    for p in pairs:
        low = jnp.where((row // 2 == col // 2) & strict, strict_part[p], 0.0)
        inverse[p] = jnp.where(eye, 1.0, -low)
    width = 2
    while width < CH:
        mask = (row // (2 * width) == col // (2 * width)) & (row // width > col // width)
        inner = {}
        held = {}
        for p in pairs:
            held[p] = split(inverse[p])
            inner[p] = mm3(split(jnp.where(mask, strict_part[p], 0.0)), held[p])
        for p in pairs:
            inverse[p] = inverse[p] - mm3(held[p], split(inner[p]))
        width *= 2

    step, solved = {}, {}
    for n, h in pairs:
        value = v_ref[n * CH : (n + 1) * CH, h * DV : (h + 1) * DV].astype(F32)
        sides = jnp.concatenate([keys[n] * (rate[n, h] * grow[n, h]), value * rate[n, h]], axis=1)
        solved[n, h] = split(mm3(inverse[n, h], sides))
    for n, h in pairs:
        fed = mm3(split(keys[n] * tail[n, h]), solved[n, h], TN)
        step[n, h] = jnp.concatenate(
            [jnp.where(eye, end[n, h], 0.0) - fed[:, :DK], fed[:, DK:]], axis=1
        )

    prefixes = {}
    for h in range(2):
        first = compose(step[1, h], step[0, h])
        second = compose(step[3, h], step[2, h])
        whole = compose(second, first)
        xs[x, h] = whole.astype(BF16)
        prefixes[1, h] = step[0, h]
        prefixes[2, h] = first
        prefixes[3, h] = (step[2, h], first)

    along_x = Gather4(xs, x, x_right, x_left, xsend, xrecv)
    along_x.start()

    base, mapped = {}, {}
    for n, h in pairs:
        scores = qk[n] * decay[n, h]
        seen = mm3(split(scores), solved[n, h])
        effective = queries[n] * grow[n, h] - seen[:, :DK]
        if n == 0:
            base[n, h], mapped[n, h] = seen[:, DK:], effective
        else:
            ahead = prefixes[n, h]
            if n == 3:
                ahead = compose(ahead[0], ahead[1])
            through = mm3(effective, ahead)
            base[n, h], mapped[n, h] = seen[:, DK:] + through[:, DK:], through[:, :DK]

    along_x.forward()
    along_x.finish()
    along_y = Gather4(ys, y, y_right, y_left, ysend, yrecv)
    for h in range(2):
        lower = compose(xs[1, h], xs[0, h])
        upper = compose(xs[3, h], xs[2, h])
        ys[y, h] = compose(upper, lower).astype(BF16)
    along_y.start()

    state = {}
    inside = {}
    start = jnp.where(
        lax.broadcasted_iota(jnp.int32, (DK, 2 * DK), 0)
        == lax.broadcasted_iota(jnp.int32, (DK, 2 * DK), 1),
        1.0,
        0.0,
    )
    for h in range(2):
        running = jnp.where(x > 0, xs[0, h].astype(F32), start)
        for other in range(1, 3):
            running = jnp.where(x > other, compose(xs[other, h], running), running)
        inside[h] = running
    along_y.forward()
    along_y.finish()
    for h in range(2):
        running = jnp.where(y > 0, ys[0, h, :, DK:].astype(F32), 0.0)
        for other in range(1, 3):
            after = mm2(ys[other, h, :, :DK], running) + ys[other, h, :, DK:].astype(F32)
            running = jnp.where(y > other, after, running)
        state[h] = split(mm3(inside[h][:, :DK], running) + inside[h][:, DK:])

    gain = gain_ref[...]
    for n, h in pairs:
        rows, cols = slice(n * CH, (n + 1) * CH), slice(h * DV, (h + 1) * DV)
        readout = base[n, h] + mm3(mapped[n, h], state[h])
        scaled = readout * lax.rsqrt(jnp.mean(readout * readout, axis=-1, keepdims=True) + EPS)
        gate = g_ref[rows, cols].astype(F32)
        o_ref[rows, cols] = (scaled * gain * (gate / (1.0 + jnp.exp(-gate)))).astype(BF16)

    along_x.drain()
    along_y.drain()


class RingSum:
    def __init__(self, own, pair_out, pair_in, out, came, psem, rsem, ring):
        self.own, self.pair_out, self.pair_in, self.out, self.came = own, pair_out, pair_in, out, came
        self.psem, self.rsem, self.ring = psem, rsem, ring
        self.sent, self.paired = [], set()

    def pair(self, d):
        return send_to(
            self.pair_out.at[d],
            self.pair_in.at[d],
            self.psem.at[0, d],
            self.psem.at[1, d],
            "exp",
            self.ring[2],
        )

    def offer(self, d):
        copy = self.pair(d)
        copy.start()
        self.sent.append(copy)

    def chip_sum(self, d, half):
        if d not in self.paired:
            self.pair(d).wait_recv()
            self.paired.add(d)
        cols = slice(half * HALF, (half + 1) * HALF)
        return self.own[d, :, cols] + self.pair_in[d, :, cols].astype(F32)

    def hop(self, way, step, half):
        return send_to(
            self.out.at[way, step, half],
            self.came.at[way, step, half],
            self.rsem.at[0, way, step, half],
            self.rsem.at[1, way, step, half],
            "exp",
            self.ring[way],
        )

    def run(self):
        for step in range(4):
            for turn in range(2):
                for way in range(2):
                    half = way if turn == 0 else 1 - way
                    if step == 0 and turn == 1:
                        continue
                    d = 4 - step if way == 0 else 4 + step
                    total = self.chip_sum(d, half)
                    if step >= 2 or (step == 1 and turn == 0):
                        self.hop(way, step - 1, half).wait_recv()
                        total = total + self.came[way, step - 1, half].astype(F32)
                    self.out[way, step, half] = total.astype(BF16)
                    copy = self.hop(way, step, half)
                    copy.start()
                    self.sent.append(copy)

    def result(self, half):
        total = self.chip_sum(0, half)
        for way in range(2):
            self.hop(way, 3, half).wait_recv()
            total = total + self.came[way, 3, half].astype(F32)
        return total

    def drain(self):
        for copy in self.sent:
            copy.wait_send()


def exp_kernel(
    mix_ref,
    hid_ref,
    ids_ref,
    route_ref,
    post_ref,
    ow_hbm,
    gw_hbm,
    uw_hbm,
    dw_hbm,
    o_ref,
    ow,
    gw,
    uw,
    dw,
    own,
    pair_out,
    pair_in,
    out,
    came,
    res,
    low,
    high,
    wsem,
    psem,
    rsem,
    gsem,
    bsem,
):
    place = lax.axis_index("exp")
    z, core = lax.div(place, 2), lax.rem(place, 2)
    right = lax.rem(z + 1, 8) * 2 + core
    left = lax.rem(z + 7, 8) * 2 + core
    sibling = z * 2 + (1 - core)
    ring = (right, left, sibling)
    loads = [
        pltpu.make_async_copy(src, dst, wsem.at[i])
        for i, (src, dst) in enumerate(((ow_hbm, ow), (gw_hbm, gw), (uw_hbm, uw), (dw_hbm, dw)))
    ]
    for load in loads:
        load.start()
    greet("exp", ring)
    loads[0].wait()

    first = RingSum(
        own.at[0],
        pair_out.at[0],
        pair_in.at[0],
        out.at[0],
        came.at[0],
        psem.at[0],
        rsem.at[0],
        ring,
    )
    weight = ow[...]
    for d in (4, 3, 5, 2, 6, 1, 7, 0):
        chip = lax.rem(z + d, 8)
        for mine in (False, True):
            part = core if mine else 1 - core
            rows = pl.ds(pl.multiple_of(chip * 64 + part * 32, 32), 32)
            block = mm(mix_ref[rows, :], weight)
            if mine:
                own[0, d] = block
            else:
                pair_out[0, d] = block.astype(BF16)
                first.offer(d)
    first.run()
    for half in range(2):
        cols = slice(half * HALF, (half + 1) * HALF)
        res[:, cols] = hid_ref[:, cols].astype(F32) + first.result(half)

    residual = res[...]
    normed = (
        residual
        * lax.rsqrt(jnp.mean(residual * residual, axis=-1, keepdims=True) + EPS)
        * post_ref[...]
    ).astype(BF16)
    low[0, 0, :, :HALF] = normed[:, :HALF]
    high[0, 0] = normed[:, HALF:]
    lane = lax.broadcasted_iota(jnp.int32, (32, 128), 1)
    table = jnp.zeros((32, 128), F32)
    for j in range(4):
        table = table + jnp.where(
            lane == ids_ref[:, j : j + 1], route_ref[:, j : j + 1].astype(F32), 0.0
        )
    low[0, 0, :, HALF:] = table.astype(BF16)

    halves = (low, high)
    sent = []

    def onward(way, step, half):
        src = (8 - step) % 8 if way == 0 else step
        dst = 7 - step if way == 0 else step + 1
        return send_to(
            halves[half].at[src, 0],
            halves[half].at[dst, 0],
            gsem.at[0, way, step, half],
            gsem.at[1, way, step, half],
            "exp",
            ring[way],
        )

    def across(d, half):
        return send_to(
            halves[half].at[d, 0],
            halves[half].at[d, 1],
            bsem.at[0, d, half],
            bsem.at[1, d, half],
            "exp",
            sibling,
        )

    def begin(copy):
        copy.start()
        sent.append(copy)

    second = RingSum(
        own.at[1],
        pair_out.at[1],
        pair_in.at[1],
        out.at[1],
        came.at[1],
        psem.at[1],
        rsem.at[1],
        ring,
    )

    def expert(offsets):
        for d in offsets:
            for half in range(2):
                across(d, half).wait_recv()
        cells = [(d, side) for d in offsets for side in range(2)]
        left_part = jnp.concatenate([low[d, side, :, :HALF] for d, side in cells], axis=0)
        right_part = jnp.concatenate([high[d, side] for d, side in cells], axis=0)
        gate = mm(left_part, gw[0, :HALF, :]) + mm(right_part, gw[0, HALF:, :])
        up = mm(left_part, uw[0, :HALF, :]) + mm(right_part, uw[0, HALF:, :])
        hidden = (gate / (1.0 + jnp.exp(-gate)) * up).astype(BF16)
        produced = mm(hidden, dw[0]).astype(BF16).astype(F32)
        for i, (d, side) in enumerate(cells):
            share = jnp.sum(
                jnp.where(lane == place, low[d, side, :, HALF:].astype(F32), 0.0),
                axis=1,
                keepdims=True,
            )
            block = produced[32 * i : 32 * i + 32] * share
            if side == 0:
                own[1, d] = block
            else:
                pair_out[1, d] = block.astype(BF16)
                second.offer(d)

    for way in range(2):
        for half in (way, 1 - way):
            begin(onward(way, 0, half))
    for half in range(2):
        begin(across(0, half))
    for load in loads[1:]:
        load.wait()
    expert((0,))
    for step in range(1, 4):
        for turn in range(2):
            for way in range(2):
                half = way if turn == 0 else 1 - way
                onward(way, step - 1, half).wait_recv()
                if step < 3 or turn == 0:
                    begin(onward(way, step, half))
                begin(across(8 - step if way == 0 else step, half))
        expert((8 - step, step))
    for way in range(2):
        onward(way, 3, way).wait_recv()
        begin(across(4, way))
    expert((4,))
    second.run()
    for half in range(2):
        cols = slice(half * HALF, (half + 1) * HALF)
        o_ref[:, cols] = (res[:, cols] + second.result(half)).astype(BF16)
    for copy in sent:
        copy.wait_send()
    first.drain()
    second.drain()


def in_vmem(count):
    return [pl.BlockSpec(memory_space=pltpu.VMEM)] * count


def seq_stage(q, k, v, g, ld, wr, gain):
    slots = pltpu.VMEM((4, 2, DK, 2 * DK), BF16)
    return pl.pallas_call(
        seq_kernel,
        out_shape=jax.ShapeDtypeStruct(v.shape, BF16),
        in_specs=in_vmem(7),
        out_specs=pl.BlockSpec(memory_space=pltpu.VMEM),
        scratch_shapes=[slots, slots] + [pltpu.SemaphoreType.DMA((4,))] * 4,
        compiler_params=pltpu.CompilerParams(
            collective_id=0, has_side_effects=True, vmem_limit_bytes=48 * 1024 * 1024
        ),
        name="seq_stage",
    )(q, k, v, g, ld, wr, gain)


def exp_stage(mixed, hidden, ids, route, post, ow, gw, uw, dw):
    scratch = [
        pltpu.VMEM(ow.shape, BF16),
        pltpu.VMEM(gw.shape, BF16),
        pltpu.VMEM(uw.shape, BF16),
        pltpu.VMEM(dw.shape, BF16),
        pltpu.VMEM((2, 8, 32, D), F32),
        pltpu.VMEM((2, 8, 32, D), BF16),
        pltpu.VMEM((2, 8, 32, D), BF16),
        pltpu.VMEM((2, 2, 4, 2, 32, HALF), BF16),
        pltpu.VMEM((2, 2, 4, 2, 32, HALF), BF16),
        pltpu.VMEM((32, D), F32),
        pltpu.VMEM((8, 2, 32, HALF + 128), BF16),
        pltpu.VMEM((8, 2, 32, HALF), BF16),
        pltpu.SemaphoreType.DMA((4,)),
        pltpu.SemaphoreType.DMA((2, 2, 8)),
        pltpu.SemaphoreType.DMA((2, 2, 2, 4, 2)),
        pltpu.SemaphoreType.DMA((2, 2, 4, 2)),
        pltpu.SemaphoreType.DMA((2, 8, 2)),
    ]
    return pl.pallas_call(
        exp_kernel,
        out_shape=jax.ShapeDtypeStruct(hidden.shape, BF16),
        in_specs=in_vmem(5) + [pl.BlockSpec(memory_space=pl.ANY)] * 4,
        out_specs=pl.BlockSpec(memory_space=pltpu.VMEM),
        scratch_shapes=scratch,
        compiler_params=pltpu.CompilerParams(
            collective_id=1, has_side_effects=True, vmem_limit_bytes=56 * 1024 * 1024
        ),
        name="exp_stage",
    )(mixed, hidden, ids, route, post, ow, gw, uw, dw)


def per_device(
    hidden_in,
    query_proj,
    key_proj,
    value_proj,
    gate_proj,
    log_decay,
    write_rate,
    head_gain,
    out_weight,
    post_gain,
    expert_ids,
    route_weight,
    gate_weight,
    up_weight,
    down_weight,
):
    mixed = seq_stage(
        query_proj,
        key_proj,
        value_proj,
        gate_proj,
        log_decay,
        write_rate,
        head_gain.reshape(1, DV),
    )
    return exp_stage(
        mixed,
        hidden_in,
        expert_ids,
        route_weight,
        post_gain.reshape(1, D),
        out_weight,
        gate_weight,
        up_weight,
        down_weight,
    )


def solution(mesh):
    in_specs = (
        P(("seq", "exp"), None),
        P("seq", "exp"),
        P("seq", "exp"),
        P("seq", "exp"),
        P("seq", "exp"),
        P("exp", "seq"),
        P("exp", "seq"),
        P(),
        P("exp", None),
        P(),
        P(("seq", "exp"), None),
        P(("seq", "exp"), None),
        P("exp", None, None),
        P("exp", None, None),
        P("exp", None, None),
    )
    out_specs = P(("seq", "exp"), None)
    return jax.shard_map(
        per_device, mesh=mesh, in_specs=in_specs, out_specs=out_specs, check_vma=False
    )
```

time: 398 us -> 104 us (0.26)
  waiting for transfers between devices: 189 us -> 0 us
  Pallas kernels: 0 us -> 91.8 us
  other arithmetic: 91.6 us -> 0 us
  matrix products: 40.5 us -> 0 us
  blocking collectives: 31.3 us -> 0 us
  between operations: 13.5 us -> 0.03 us
  local copies, waits for them, and re-layouts: 22.7 us -> 10.7 us
  starting transfers between devices: 4.41 us -> 0 us
    all_gather x2 -> x0, waiting for transfers between devices: 93 us -> none  [prefix(): lax.all_gather(a.astype(kind), axis)]
    pallas_call x0 -> x2, Pallas kernels: none -> 91.8 us  [the longest x1 64 us: exp_stage(): pl.pallas_call(exp_kernel, out_shape=jax.ShapeDtypeStruct(hidden.shape, B...]
    another operation x7 -> x0, other arithmetic: 80.9 us -> none  [the longest x3 80.1 us: recurrent_mix(): jax.scipy.linalg.solve_triangular(unit_lower, right_sides, lower=True, un...]
    reduce_scatter x1 -> x0, waiting for transfers between devices: 69.5 us -> none  [per_device(): lax.psum_scatter(jnp.dot(picked, out_weight, preferred_element_type=jnp.f...]
    dot_general x23 -> x0, matrix products: 39.5 us -> none  [the longest x4 7.62 us: fold_block(): jnp.einsum('jbe,jew->jbw', block_transform, cumulative_bias, precision=HI...]
    all_to_all x1 -> x0, blocking collectives: 31.3 us -> none  [per_device(): lax.all_to_all(outgoing, 'exp', split_axis=0, concat_axis=0, tiled=True)]
    all_to_all x1 -> x0, waiting for transfers between devices: 26.5 us -> none  [per_device(): lax.all_to_all(produced, 'exp', split_axis=0, concat_axis=0, tiled=True)]
    unnamed x27 -> x19, local copies, waits for them, and re-layouts: 2.47 us -> 10.7 us
  transfers between devices with their start and end apart: 4 -> 0, of which waited for: 4 -> 0; matrix products, arithmetic and copies ran while one was open for 2% -> 0% of each run, Pallas kernels for 0% -> 0%
where the time goes in v1:
time: 104 us; the launch traced here: 103 us
  Pallas kernels  91.8 us (88%)
  local copies, waits for them, and re-layouts  10.7 us (10%)
    pallas_call x1, Pallas kernels, exp_stage(): pl.pallas_call(exp_kernel, out_shape=jax.ShapeDtypeStruct(hidden.shape, B...  64 us
    pallas_call x1, Pallas kernels, seq_stage(): pl.pallas_call(seq_kernel, out_shape=jax.ShapeDtypeStruct(v.shape, BF16),...  27.7 us
    unnamed x19, local copies, waits for them, and re-layouts  10.7 us

profile of v1, /device:TPU:8, one launch (start us, length us, event | category | flops | bytes accessed | tf_op | source)
XLA Modules:
  0.0 102.5 jit_solution(7129237612774450507)
XLA Ops:
  0.0 1.4 %copy.17.route_ref = bf16[32,4]{1,0:T(8,128)(2,1)} copy(bf16[32,4]{0,1:T(4,128)(2,1)} %param.26) | data formatting | bytes 512 | tf_op args[11]
  1.4 1.4 %copy.16.ids_ref = s32[32,4]{1,0:T(8,128)} copy(s32[32,4]{0,1:T(4,128)} %param.25) | data formatting | bytes 1024 | tf_op args[10]
  2.7 0.0 copy-start.1
  2.7 0.9 copy-done.1
  3.7 0.0 copy-start.2
  3.7 0.9 copy-done.2
  4.6 0.0 copy-start.3
  4.6 0.9 copy-done.3
  5.5 0.0 copy-start.4
  5.5 0.9 copy-done.4
  6.4 0.0 copy-start.5
  6.4 0.7 copy-done.5
  7.1 0.0 copy-start.6
  7.1 0.7 copy-done.6
  7.8 0.0 copy-start.7
  7.8 0.7 copy-done.7
  8.5 27.7 %seq_stage.1.mix_ref = bf16[512,256]{1,0:T(8,128)(2,1)S(1)} custom-call(bf16[512,128]{1,0:T(8,128)(2,1)S(1)} %copy-done.3, bf16[512,128]{1,0:T(8,128)(2,1)S(1)} %copy-done.4, bf16[512,256]{1,0:T(8,128)(2,1)S(1)} %copy-done.1, bf16[512,256]{1,0:T(8,128)(2,1)S(1)} %copy-done.2, f32[2,512]{1,0:T(2,128)S(1)} %copy-done.5, f32[2,512]{1,0:T(2,128)S(1)} %copy-done.6, ...), custom_call_target="tpu_custom_call" | custom-call | tf_op jit(solution)/shard_map/seq_stage/pallas_call | solution.py:522
  36.2 0.0 copy-start
  36.2 0.7 copy-done
  36.9 64.0 %exp_stage.1 = bf16[32,2048]{1,0:T(8,128)(2,1)} custom-call(bf16[512,256]{1,0:T(8,128)(2,1)} %copy-done, bf16[32,2048]{1,0:T(8,128)(2,1)} %hid_ref.1, s32[32,4]{1,0:T(8,128)} %copy.16.ids_ref, bf16[32,4]{1,0:T(8,128)(2,1)} %copy.17.route_ref, f32[1,2048]{1,0:T(1,128)} %bitcast.3, bf16[256,2048]{1,0:T(8,128)(2,1)} %ow_hbm.1, bf16[1,2048,512]{2,1,0:T(8,128)(2,1)} %gw_hbm.1, ...), custom_call_target="tpu_custom_call" | custom-call | tf_op jit(solution)/shard_map/exp_stage/pallas_call | solution.py:555
  101.0 1.6 %copy.19 = bf16[32,2048]{1,0:T(8,128)(2,1)} copy(bf16[32,2048]{1,0:T(8,128)(2,1)} %exp_stage.1) | data formatting | bytes 262144
Async XLA Ops:
  2.7 0.9 copy-start.1
  3.7 0.9 copy-start.2
  4.6 0.9 copy-start.3
  5.5 0.9 copy-start.4
  6.4 0.7 copy-start.5
  7.1 0.7 copy-start.6
  7.8 0.7 copy-start.7
  36.2 0.7 copy-start

commit v2 on v1

--- a/solution.py
+++ b/solution.py
@@ -42,11 +42,11 @@
     return mm(a, bh, dims) + mm(a, bl, dims)
 
 
-def greet(axis, peers):
+def greet(peers):
     barrier = pltpu.get_barrier_semaphore()
-    for peer in peers:
+    for axis, peer in peers:
         pl.semaphore_signal(barrier, inc=1, device_id={axis: peer}, device_id_type=MESH)
-    pl.semaphore_wait(barrier, len(peers))
+    return lambda: pl.semaphore_wait(barrier, len(peers))
 
 
 def send_to(src, dst, send_sem, recv_sem, axis, peer):
@@ -108,28 +108,9 @@
     return joined + jnp.concatenate([jnp.zeros((DK, DK), F32), later[:, DK:]], axis=1)
 
 
-def seq_kernel(
-    q_ref,
-    k_ref,
-    v_ref,
-    g_ref,
-    ld_ref,
-    wr_ref,
-    gain_ref,
-    o_ref,
-    xs,
-    ys,
-    xsend,
-    xrecv,
-    ysend,
-    yrecv,
-):
-    place = lax.axis_index("seq")
-    x, y = lax.rem(place, 4), lax.div(place, 4)
-    x_right, x_left = y * 4 + lax.rem(x + 1, 4), y * 4 + lax.rem(x + 3, 4)
-    y_right, y_left = lax.rem(y + 1, 4) * 4 + x, lax.rem(y + 3, 4) * 4 + x
-    greet("seq", (x_right, x_left, y_right, y_left))
-
+def seq_part(q_ref, k_ref, v_ref, g_ref, ld_ref, wr_ref, gain_ref, o_ref, xs, ys, sems, at, meet, late):
+    xsend, xrecv, ysend, yrecv = sems
+    x, y, x_right, x_left, y_right, y_left = at
     chunks = q_ref.shape[0] // CH
     row = lax.broadcasted_iota(jnp.int32, (CH, CH), 0)
     col = lax.broadcasted_iota(jnp.int32, (CH, CH), 1)
@@ -204,6 +185,7 @@
         prefixes[2, h] = first
         prefixes[3, h] = (step[2, h], first)
 
+    meet()
     along_x = Gather4(xs, x, x_right, x_left, xsend, xrecv)
     along_x.start()
 
@@ -252,6 +234,7 @@
             running = jnp.where(y > other, after, running)
         state[h] = split(mm3(inside[h][:, :DK], running) + inside[h][:, DK:])
 
+    late()
     gain = gain_ref[...]
     for n, h in pairs:
         rows, cols = slice(n * CH, (n + 1) * CH), slice(h * DV, (h + 1) * DV)
@@ -260,8 +243,12 @@
         gate = g_ref[rows, cols].astype(F32)
         o_ref[rows, cols] = (scaled * gain * (gate / (1.0 + jnp.exp(-gate)))).astype(BF16)
 
-    along_x.drain()
-    along_y.drain()
+
+    def drain():
+        along_x.drain()
+        along_y.drain()
+
+    return drain
 
 
 class RingSum:
@@ -331,49 +318,47 @@
             copy.wait_send()
 
 
-def exp_kernel(
-    mix_ref,
-    hid_ref,
-    ids_ref,
-    route_ref,
-    post_ref,
-    ow_hbm,
-    gw_hbm,
-    uw_hbm,
-    dw_hbm,
-    o_ref,
-    ow,
-    gw,
-    uw,
-    dw,
-    own,
-    pair_out,
-    pair_in,
-    out,
-    came,
-    res,
-    low,
-    high,
-    wsem,
-    psem,
-    rsem,
-    gsem,
-    bsem,
-):
+def kernel(*refs):
+    inputs, o_ref, scratch = refs[:15], refs[15], refs[16:]
+    held, scratch = scratch[:15], scratch[15:]
+    (own, pair_out, pair_in, out, came, res, low, high, mix_ref, xs, ys) = scratch[:11]
+    (wsem, psem, rsem, gsem, bsem, *seq_sems) = scratch[11:]
+    (hid_ref, q, k, v, g, ld, wr, gain, ow, post_ref, ids_ref, route_ref, gw, uw, dw) = held
+    loads = [
+        pltpu.make_async_copy(src, dst, wsem.at[i])
+        for i, (src, dst) in enumerate(zip(inputs, held))
+    ]
+    early, middle = (2, 1, 5, 6, 3), (4, 7, 8, 0, 9, 10, 11)
+    for i in early:
+        loads[i].start()
+
     place = lax.axis_index("exp")
     z, core = lax.div(place, 2), lax.rem(place, 2)
     right = lax.rem(z + 1, 8) * 2 + core
     left = lax.rem(z + 7, 8) * 2 + core
     sibling = z * 2 + (1 - core)
     ring = (right, left, sibling)
-    loads = [
-        pltpu.make_async_copy(src, dst, wsem.at[i])
-        for i, (src, dst) in enumerate(((ow_hbm, ow), (gw_hbm, gw), (uw_hbm, uw), (dw_hbm, dw)))
-    ]
-    for load in loads:
-        load.start()
-    greet("exp", ring)
-    loads[0].wait()
+    turn_at = lax.axis_index("seq")
+    x, y = lax.rem(turn_at, 4), lax.div(turn_at, 4)
+    at = (
+        x,
+        y,
+        y * 4 + lax.rem(x + 1, 4),
+        y * 4 + lax.rem(x + 3, 4),
+        lax.rem(y + 1, 4) * 4 + x,
+        lax.rem(y + 3, 4) * 4 + x,
+    )
+    meet = greet([("seq", peer) for peer in at[2:]] + [("exp", peer) for peer in ring])
+    for i in early:
+        loads[i].wait()
+    for i in middle + (12, 13, 14):
+        loads[i].start()
+
+    def late():
+        for i in middle:
+            loads[i].wait()
+
+    drain_seq = seq_part(q, k, v, g, ld, wr, gain, mix_ref, xs, ys, seq_sems, at, meet, late)
 
     first = RingSum(
         own.at[0],
@@ -412,10 +397,17 @@
     high[0, 0] = normed[:, HALF:]
     lane = lax.broadcasted_iota(jnp.int32, (32, 128), 1)
     table = jnp.zeros((32, 128), F32)
+    ids = ids_ref[...].astype(F32)
+    routes = route_ref[...].astype(F32)
+    same = lax.broadcasted_iota(jnp.int32, (32, 32), 0) == lax.broadcasted_iota(
+        jnp.int32, (32, 32), 1
+    )
     for j in range(4):
-        table = table + jnp.where(
-            lane == ids_ref[:, j : j + 1], route_ref[:, j : j + 1].astype(F32), 0.0
+        named, share = (
+            jnp.sum(jnp.where(same, a[j : j + 1, :], 0.0), axis=1, keepdims=True)
+            for a in (ids, routes)
         )
+        table = table + jnp.where(lane.astype(F32) == named, share, 0.0)
     low[0, 0, :, HALF:] = table.astype(BF16)
 
     halves = (low, high)
@@ -487,7 +479,7 @@
             begin(onward(way, 0, half))
     for half in range(2):
         begin(across(0, half))
-    for load in loads[1:]:
+    for load in loads[12:]:
         load.wait()
     expert((0,))
     for step in range(1, 4):
@@ -511,33 +503,17 @@
         copy.wait_send()
     first.drain()
     second.drain()
-
-
-def in_vmem(count):
-    return [pl.BlockSpec(memory_space=pltpu.VMEM)] * count
-
-
-def seq_stage(q, k, v, g, ld, wr, gain):
+    drain_seq()
+
+
+def per_device(*args):
+    args = list(args)
+    args[7] = args[7].reshape(1, DV)
+    args[9] = args[9].reshape(1, D)
+    args[10] = args[10].T
+    args[11] = args[11].T
     slots = pltpu.VMEM((4, 2, DK, 2 * DK), BF16)
-    return pl.pallas_call(
-        seq_kernel,
-        out_shape=jax.ShapeDtypeStruct(v.shape, BF16),
-        in_specs=in_vmem(7),
-        out_specs=pl.BlockSpec(memory_space=pltpu.VMEM),
-        scratch_shapes=[slots, slots] + [pltpu.SemaphoreType.DMA((4,))] * 4,
-        compiler_params=pltpu.CompilerParams(
-            collective_id=0, has_side_effects=True, vmem_limit_bytes=48 * 1024 * 1024
-        ),
-        name="seq_stage",
-    )(q, k, v, g, ld, wr, gain)
-
-
-def exp_stage(mixed, hidden, ids, route, post, ow, gw, uw, dw):
-    scratch = [
-        pltpu.VMEM(ow.shape, BF16),
-        pltpu.VMEM(gw.shape, BF16),
-        pltpu.VMEM(uw.shape, BF16),
-        pltpu.VMEM(dw.shape, BF16),
+    scratch = [pltpu.VMEM(a.shape, a.dtype) for a in args] + [
         pltpu.VMEM((2, 8, 32, D), F32),
         pltpu.VMEM((2, 8, 32, D), BF16),
         pltpu.VMEM((2, 8, 32, D), BF16),
@@ -546,62 +522,26 @@
         pltpu.VMEM((32, D), F32),
         pltpu.VMEM((8, 2, 32, HALF + 128), BF16),
         pltpu.VMEM((8, 2, 32, HALF), BF16),
-        pltpu.SemaphoreType.DMA((4,)),
+        pltpu.VMEM(args[3].shape, BF16),
+        slots,
+        slots,
+        pltpu.SemaphoreType.DMA((15,)),
         pltpu.SemaphoreType.DMA((2, 2, 8)),
         pltpu.SemaphoreType.DMA((2, 2, 2, 4, 2)),
         pltpu.SemaphoreType.DMA((2, 2, 4, 2)),
         pltpu.SemaphoreType.DMA((2, 8, 2)),
     ]
     return pl.pallas_call(
-        exp_kernel,
-        out_shape=jax.ShapeDtypeStruct(hidden.shape, BF16),
-        in_specs=in_vmem(5) + [pl.BlockSpec(memory_space=pl.ANY)] * 4,
+        kernel,
+        out_shape=jax.ShapeDtypeStruct(args[0].shape, BF16),
+        in_specs=[pl.BlockSpec(memory_space=pl.ANY)] * 15,
         out_specs=pl.BlockSpec(memory_space=pltpu.VMEM),
-        scratch_shapes=scratch,
+        scratch_shapes=scratch + [pltpu.SemaphoreType.DMA((4,))] * 4,
         compiler_params=pltpu.CompilerParams(
-            collective_id=1, has_side_effects=True, vmem_limit_bytes=56 * 1024 * 1024
+            collective_id=0, has_side_effects=True, vmem_limit_bytes=62 * 1024 * 1024
         ),
-        name="exp_stage",
-    )(mixed, hidden, ids, route, post, ow, gw, uw, dw)
-
-
-def per_device(
-    hidden_in,
-    query_proj,
-    key_proj,
-    value_proj,
-    gate_proj,
-    log_decay,
-    write_rate,
-    head_gain,
-    out_weight,
-    post_gain,
-    expert_ids,
-    route_weight,
-    gate_weight,
-    up_weight,
-    down_weight,
-):
-    mixed = seq_stage(
-        query_proj,
-        key_proj,
-        value_proj,
-        gate_proj,
-        log_decay,
-        write_rate,
-        head_gain.reshape(1, DV),
-    )
-    return exp_stage(
-        mixed,
-        hidden_in,
-        expert_ids,
-        route_weight,
-        post_gain.reshape(1, D),
-        out_weight,
-        gate_weight,
-        up_weight,
-        down_weight,
-    )
+        name="layer",
+    )(*args)
 
 
 def solution(mesh):

time: 104 us -> 91.9 us (0.88)
  local copies, waits for them, and re-layouts: 10.7 us -> 1.57 us
  Pallas kernels: 91.8 us -> 89.5 us
    unnamed x19 -> x1, local copies, waits for them, and re-layouts: 10.7 us -> 1.57 us
    pallas_call x2 -> x1, Pallas kernels: 91.8 us -> 89.5 us  [per_device(): pl.pallas_call(kernel, out_shape=jax.ShapeDtypeStruct(args[0].shape, BF16...]
where the time goes in v2:
time: 91.9 us; the launch traced here: 91.1 us
  Pallas kernels  89.5 us (97%)
  local copies, waits for them, and re-layouts  1.57 us (2%)
    pallas_call x1, Pallas kernels, per_device(): pl.pallas_call(kernel, out_shape=jax.ShapeDtypeStruct(args[0].shape, BF16...  89.5 us

profile of v2, /device:TPU:8, one launch (start us, length us, event | category | flops | bytes accessed | tf_op | source)
XLA Modules:
  0.0 91.1 jit_solution(5213451856732696647)
XLA Ops:
  0.0 89.5 %layer.1 = bf16[32,2048]{1,0:T(8,128)(2,1)} custom-call(bf16[32,2048]{1,0:T(8,128)(2,1)} %refs_0_.1, bf16[512,128]{1,0:T(8,128)(2,1)} %refs_1_.1, bf16[512,128]{1,0:T(8,128)(2,1)} %refs_2_.1, bf16[512,256]{1,0:T(8,128)(2,1)} %refs_3_.1, bf16[512,256]{1,0:T(8,128)(2,1)} %refs_4_.1, f32[2,512]{1,0:T(2,128)} %refs_5_.1, f32[2,512]{1,0:T(2,128)} %refs_6_.1, ...), custom_call_target="tpu_custom_call" | custom-call | tf_op jit(solution)/shard_map/layer/pallas_call | solution.py:534
  89.5 1.6 %copy.17 = bf16[32,2048]{1,0:T(8,128)(2,1)} copy(bf16[32,2048]{1,0:T(8,128)(2,1)} %layer.1) | data formatting | bytes 262144

commit v3 on v2

--- a/solution.py
+++ b/solution.py
@@ -13,7 +13,8 @@
 DV = 128
 EPS = 1e-06
 CH = 128
-HALF = D // 2
+PARTS = 4
+WIDE = D // PARTS
 F32 = jnp.float32
 BF16 = jnp.bfloat16
 MESH = pl.DeviceIdType.MESH
@@ -108,7 +109,7 @@
     return joined + jnp.concatenate([jnp.zeros((DK, DK), F32), later[:, DK:]], axis=1)
 
 
-def seq_part(q_ref, k_ref, v_ref, g_ref, ld_ref, wr_ref, gain_ref, o_ref, xs, ys, sems, at, meet, late):
+def seq_part(q_ref, k_ref, v_ref, g_ref, ld_ref, wr_ref, gain_ref, mix, xs, ys, sems, at, late, ready):
     xsend, xrecv, ysend, yrecv = sems
     x, y, x_right, x_left, y_right, y_left = at
     chunks = q_ref.shape[0] // CH
@@ -185,7 +186,6 @@
         prefixes[2, h] = first
         prefixes[3, h] = (step[2, h], first)
 
-    meet()
     along_x = Gather4(xs, x, x_right, x_left, xsend, xrecv)
     along_x.start()
 
@@ -236,13 +236,18 @@
 
     late()
     gain = gain_ref[...]
-    for n, h in pairs:
-        rows, cols = slice(n * CH, (n + 1) * CH), slice(h * DV, (h + 1) * DV)
-        readout = base[n, h] + mm3(mapped[n, h], state[h])
-        scaled = readout * lax.rsqrt(jnp.mean(readout * readout, axis=-1, keepdims=True) + EPS)
-        gate = g_ref[rows, cols].astype(F32)
-        o_ref[rows, cols] = (scaled * gain * (gate / (1.0 + jnp.exp(-gate)))).astype(BF16)
-
+    for h in range(2):
+        cols = slice(h * DV, (h + 1) * DV)
+        for n in range(chunks):
+            rows = slice(n * CH, (n + 1) * CH)
+            readout = base[n, h] + mm3(mapped[n, h], state[h])
+            scaled = readout * lax.rsqrt(jnp.mean(readout * readout, axis=-1, keepdims=True) + EPS)
+            gate = g_ref[rows, cols].astype(F32)
+            mixed = (scaled * gain * (gate / (1.0 + jnp.exp(-gate)))).astype(BF16)
+            for i in range(4):
+                at_chip = (2 * n + i // 2) * 32
+                mix[i % 2, h, at_chip : at_chip + 32] = mixed[32 * i : 32 * i + 32]
+        ready(h)
 
     def drain():
         along_x.drain()
@@ -252,65 +257,42 @@
 
 
 class RingSum:
-    def __init__(self, own, pair_out, pair_in, out, came, psem, rsem, ring):
-        self.own, self.pair_out, self.pair_in, self.out, self.came = own, pair_out, pair_in, out, came
-        self.psem, self.rsem, self.ring = psem, rsem, ring
-        self.sent, self.paired = [], set()
-
-    def pair(self, d):
+    def __init__(self, own, out, came, sem, ring):
+        self.own, self.out, self.came, self.sem, self.ring = own, out, came, sem, ring
+        self.sent = []
+
+    def hop(self, way, step, part):
         return send_to(
-            self.pair_out.at[d],
-            self.pair_in.at[d],
-            self.psem.at[0, d],
-            self.psem.at[1, d],
-            "exp",
-            self.ring[2],
-        )
-
-    def offer(self, d):
-        copy = self.pair(d)
-        copy.start()
-        self.sent.append(copy)
-
-    def chip_sum(self, d, half):
-        if d not in self.paired:
-            self.pair(d).wait_recv()
-            self.paired.add(d)
-        cols = slice(half * HALF, (half + 1) * HALF)
-        return self.own[d, :, cols] + self.pair_in[d, :, cols].astype(F32)
-
-    def hop(self, way, step, half):
-        return send_to(
-            self.out.at[way, step, half],
-            self.came.at[way, step, half],
-            self.rsem.at[0, way, step, half],
-            self.rsem.at[1, way, step, half],
+            self.out.at[way, step, part],
+            self.came.at[way, step, part],
+            self.sem.at[0, way, step, part],
+            self.sem.at[1, way, step, part],
             "exp",
             self.ring[way],
         )
 
-    def run(self):
+    def run(self, prepare):
         for step in range(4):
-            for turn in range(2):
-                for way in range(2):
-                    half = way if turn == 0 else 1 - way
-                    if step == 0 and turn == 1:
-                        continue
-                    d = 4 - step if way == 0 else 4 + step
-                    total = self.chip_sum(d, half)
-                    if step >= 2 or (step == 1 and turn == 0):
-                        self.hop(way, step - 1, half).wait_recv()
-                        total = total + self.came[way, step - 1, half].astype(F32)
-                    self.out[way, step, half] = total.astype(BF16)
-                    copy = self.hop(way, step, half)
-                    copy.start()
-                    self.sent.append(copy)
-
-    def result(self, half):
-        total = self.chip_sum(0, half)
+            prepare(step)
+            for turn, way, part in turns():
+                if step == 0 and turn == 1:
+                    continue
+                d = 4 - step if way == 0 else 4 + step
+                total = self.own[d, :, part * WIDE : (part + 1) * WIDE]
+                if step >= 2 or (step == 1 and turn == 0):
+                    self.hop(way, step - 1, part).wait_recv()
+                    total = total + self.came[way, step - 1, part].astype(F32)
+                self.out[way, step, part] = total.astype(BF16)
+                copy = self.hop(way, step, part)
+                copy.start()
+                self.sent.append(copy)
+        prepare(4)
+
+    def result(self, part):
+        total = self.own[0, :, part * WIDE : (part + 1) * WIDE]
         for way in range(2):
-            self.hop(way, 3, half).wait_recv()
-            total = total + self.came[way, 3, half].astype(F32)
+            self.hop(way, 3, part).wait_recv()
+            total = total + self.came[way, 3, part].astype(F32)
         return total
 
     def drain(self):
@@ -318,26 +300,29 @@
             copy.wait_send()
 
 
+def turns():
+    some = PARTS // 2
+    return [
+        (turn, way, (way if turn == 0 else 1 - way) * some + i)
+        for turn in range(2)
+        for i in range(some)
+        for way in range(2)
+    ]
+
+
 def kernel(*refs):
     inputs, o_ref, scratch = refs[:15], refs[15], refs[16:]
     held, scratch = scratch[:15], scratch[15:]
-    (own, pair_out, pair_in, out, came, res, low, high, mix_ref, xs, ys) = scratch[:11]
-    (wsem, psem, rsem, gsem, bsem, *seq_sems) = scratch[11:]
+    (own, out, came, res, tokens, table, mix, mix_in, xs, ys) = scratch[:10]
+    (wsem, csem, msem, tsem, rsem, gsem, *seq_sems) = scratch[10:]
     (hid_ref, q, k, v, g, ld, wr, gain, ow, post_ref, ids_ref, route_ref, gw, uw, dw) = held
-    loads = [
-        pltpu.make_async_copy(src, dst, wsem.at[i])
-        for i, (src, dst) in enumerate(zip(inputs, held))
-    ]
-    early, middle = (2, 1, 5, 6, 3), (4, 7, 8, 0, 9, 10, 11)
-    for i in early:
-        loads[i].start()
+    weights = (8, 12, 13, 14)
 
     place = lax.axis_index("exp")
     z, core = lax.div(place, 2), lax.rem(place, 2)
-    right = lax.rem(z + 1, 8) * 2 + core
-    left = lax.rem(z + 7, 8) * 2 + core
+    chips = [lax.rem(z + d, 8) * 2 + core for d in range(8)]
     sibling = z * 2 + (1 - core)
-    ring = (right, left, sibling)
+    ring = (chips[1], chips[7])
     turn_at = lax.axis_index("seq")
     x, y = lax.rem(turn_at, 4), lax.div(turn_at, 4)
     at = (
@@ -348,44 +333,112 @@
         lax.rem(y + 1, 4) * 4 + x,
         lax.rem(y + 3, 4) * 4 + x,
     )
-    meet = greet([("seq", peer) for peer in at[2:]] + [("exp", peer) for peer in ring])
+    meet = greet(
+        [("seq", peer) for peer in at[2:]] + [("exp", peer) for peer in chips[1:] + [sibling]]
+    )
+
+    loads, shared = [], []
+    for i, (src, dst) in enumerate(zip(inputs, held)):
+        if i in weights:
+            flat = src if i == 8 else src.at[0]
+            n = weights.index(i)
+            shared.append(
+                send_to(flat, dst.at[core], csem.at[0, n], csem.at[1, n], "exp", sibling)
+            )
+            dst, src = dst.at[core], flat
+        loads.append(pltpu.make_async_copy(src, dst, wsem.at[i]))
+    arriving = [
+        send_to(
+            held[i].at[1 - core], held[i].at[1 - core], csem.at[0, n], csem.at[1, n], "exp", sibling
+        )
+        for n, i in enumerate(weights)
+    ]
+    early, middle = (2, 1, 5, 6, 3), (10, 11, 4, 7, 0, 9)
+    for i in early + middle:
+        loads[i].start()
+    meet()
     for i in early:
         loads[i].wait()
-    for i in middle + (12, 13, 14):
+    for i in weights:
         loads[i].start()
+    for copy in shared:
+        copy.start()
+
+    lane = lax.broadcasted_iota(jnp.int32, (32, 128), 1).astype(F32)
+    sent = []
+
+    def begin(copy):
+        copy.start()
+        sent.append(copy)
 
     def late():
         for i in middle:
             loads[i].wait()
-
-    drain_seq = seq_part(q, k, v, g, ld, wr, gain, mix_ref, xs, ys, seq_sems, at, meet, late)
-
-    first = RingSum(
-        own.at[0],
-        pair_out.at[0],
-        pair_in.at[0],
-        out.at[0],
-        came.at[0],
-        psem.at[0],
-        rsem.at[0],
-        ring,
-    )
-    weight = ow[...]
-    for d in (4, 3, 5, 2, 6, 1, 7, 0):
-        chip = lax.rem(z + d, 8)
-        for mine in (False, True):
-            part = core if mine else 1 - core
-            rows = pl.ds(pl.multiple_of(chip * 64 + part * 32, 32), 32)
-            block = mm(mix_ref[rows, :], weight)
-            if mine:
-                own[0, d] = block
-            else:
-                pair_out[0, d] = block.astype(BF16)
-                first.offer(d)
-    first.run()
-    for half in range(2):
-        cols = slice(half * HALF, (half + 1) * HALF)
-        res[:, cols] = hid_ref[:, cols].astype(F32) + first.result(half)
+        ids = ids_ref[...].astype(F32)
+        routes = route_ref[...].astype(F32)
+        same = lax.broadcasted_iota(jnp.int32, (32, 32), 0) == lax.broadcasted_iota(
+            jnp.int32, (32, 32), 1
+        )
+        shares = jnp.zeros((32, 128), F32)
+        for j in range(4):
+            named, share = (
+                jnp.sum(jnp.where(same, a[j : j + 1, :], 0.0), axis=1, keepdims=True)
+                for a in (ids, routes)
+            )
+            shares = shares + jnp.where(lane == named, share, 0.0)
+        table[0] = shares.astype(BF16)
+        for d in range(1, 8):
+            begin(share_table(d))
+
+    def share_table(d):
+        return send_to(
+            table.at[0], table.at[8 - d], tsem.at[0, 8 - d], tsem.at[1, 8 - d], "exp", chips[d]
+        )
+
+    def mix_copy(h):
+        return send_to(
+            mix.at[1 - core, h], mix_in.at[h], msem.at[0, h], msem.at[1, h], "exp", sibling
+        )
+
+    drain_seq = seq_part(
+        q,
+        k,
+        v,
+        g,
+        ld,
+        wr,
+        gain,
+        mix,
+        xs,
+        ys,
+        seq_sems,
+        at,
+        late,
+        lambda h: begin(mix_copy(h)),
+    )
+
+    loads[8].wait()
+    arriving[0].wait_recv()
+    for h in range(2):
+        mix_copy(h).wait_recv()
+
+    def project(offsets):
+        rows = [pl.ds(pl.multiple_of(lax.rem(z + d, 8) * 32, 32), 32) for d in offsets]
+        mine, other = (
+            jnp.concatenate(
+                [jnp.concatenate([ref[h, r] for h in range(2)], axis=1) for r in rows], axis=0
+            )
+            for ref in (mix.at[core], mix_in)
+        )
+        block = mm(mine, ow[core]) + mm(other, ow[1 - core])
+        for i, d in enumerate(offsets):
+            own[0, d] = block[32 * i : 32 * i + 32]
+
+    first = RingSum(own.at[0], out.at[0], came.at[0], rsem.at[0], ring)
+    first.run(lambda step: project(((4,), (3, 5), (2, 6), (1, 7), (0,))[step]))
+    for part in range(PARTS):
+        cols = slice(part * WIDE, (part + 1) * WIDE)
+        res[:, cols] = hid_ref[:, cols].astype(F32) + first.result(part)
 
     residual = res[...]
     normed = (
@@ -393,113 +446,70 @@
         * lax.rsqrt(jnp.mean(residual * residual, axis=-1, keepdims=True) + EPS)
         * post_ref[...]
     ).astype(BF16)
-    low[0, 0, :, :HALF] = normed[:, :HALF]
-    high[0, 0] = normed[:, HALF:]
-    lane = lax.broadcasted_iota(jnp.int32, (32, 128), 1)
-    table = jnp.zeros((32, 128), F32)
-    ids = ids_ref[...].astype(F32)
-    routes = route_ref[...].astype(F32)
-    same = lax.broadcasted_iota(jnp.int32, (32, 32), 0) == lax.broadcasted_iota(
-        jnp.int32, (32, 32), 1
-    )
-    for j in range(4):
-        named, share = (
-            jnp.sum(jnp.where(same, a[j : j + 1, :], 0.0), axis=1, keepdims=True)
-            for a in (ids, routes)
-        )
-        table = table + jnp.where(lane.astype(F32) == named, share, 0.0)
-    low[0, 0, :, HALF:] = table.astype(BF16)
-
-    halves = (low, high)
-    sent = []
-
-    def onward(way, step, half):
+    for part in range(PARTS):
+        tokens[0, part] = normed[:, part * WIDE : (part + 1) * WIDE]
+
+    def onward(way, step, part):
         src = (8 - step) % 8 if way == 0 else step
         dst = 7 - step if way == 0 else step + 1
         return send_to(
-            halves[half].at[src, 0],
-            halves[half].at[dst, 0],
-            gsem.at[0, way, step, half],
-            gsem.at[1, way, step, half],
+            tokens.at[src, part],
+            tokens.at[dst, part],
+            gsem.at[0, way, step, part],
+            gsem.at[1, way, step, part],
             "exp",
             ring[way],
         )
 
-    def across(d, half):
-        return send_to(
-            halves[half].at[d, 0],
-            halves[half].at[d, 1],
-            bsem.at[0, d, half],
-            bsem.at[1, d, half],
-            "exp",
-            sibling,
-        )
-
-    def begin(copy):
-        copy.start()
-        sent.append(copy)
-
-    second = RingSum(
-        own.at[1],
-        pair_out.at[1],
-        pair_in.at[1],
-        out.at[1],
-        came.at[1],
-        psem.at[1],
-        rsem.at[1],
-        ring,
-    )
-
     def expert(offsets):
+        picked = jnp.concatenate(
+            [
+                jnp.concatenate([tokens[d, part] for part in range(PARTS)], axis=1)
+                for d in offsets
+            ],
+            axis=0,
+        )
         for d in offsets:
-            for half in range(2):
-                across(d, half).wait_recv()
-        cells = [(d, side) for d in offsets for side in range(2)]
-        left_part = jnp.concatenate([low[d, side, :, :HALF] for d, side in cells], axis=0)
-        right_part = jnp.concatenate([high[d, side] for d, side in cells], axis=0)
-        gate = mm(left_part, gw[0, :HALF, :]) + mm(right_part, gw[0, HALF:, :])
-        up = mm(left_part, uw[0, :HALF, :]) + mm(right_part, uw[0, HALF:, :])
-        hidden = (gate / (1.0 + jnp.exp(-gate)) * up).astype(BF16)
-        produced = mm(hidden, dw[0]).astype(BF16).astype(F32)
-        for i, (d, side) in enumerate(cells):
-            share = jnp.sum(
-                jnp.where(lane == place, low[d, side, :, HALF:].astype(F32), 0.0),
-                axis=1,
-                keepdims=True,
-            )
-            block = produced[32 * i : 32 * i + 32] * share
-            if side == 0:
-                own[1, d] = block
-            else:
-                pair_out[1, d] = block.astype(BF16)
-                second.offer(d)
-
-    for way in range(2):
-        for half in (way, 1 - way):
-            begin(onward(way, 0, half))
-    for half in range(2):
-        begin(across(0, half))
-    for load in loads[12:]:
-        load.wait()
-    expert((0,))
+            if d > 0:
+                share_table(8 - d).wait_recv()
+        shares = jnp.concatenate([table[d] for d in offsets], axis=0).astype(F32)
+        lanes = lax.broadcasted_iota(jnp.int32, shares.shape, 1)
+        total = None
+        for e in range(2):
+            gate = mm(picked, gw[e])
+            up = mm(picked, uw[e])
+            hidden = (gate / (1.0 + jnp.exp(-gate)) * up).astype(BF16)
+            produced = mm(hidden, dw[e]).astype(BF16).astype(F32)
+            share = jnp.sum(jnp.where(lanes == z * 2 + e, shares, 0.0), axis=1, keepdims=True)
+            total = produced * share if total is None else total + produced * share
+        for i, d in enumerate(offsets):
+            own[1, d] = total[32 * i : 32 * i + 32]
+
+    for turn, way, part in turns():
+        begin(onward(way, 0, part))
+    for i in weights[1:]:
+        loads[i].wait()
+    for copy in arriving[1:]:
+        copy.wait_recv()
     for step in range(1, 4):
-        for turn in range(2):
-            for way in range(2):
-                half = way if turn == 0 else 1 - way
-                onward(way, step - 1, half).wait_recv()
-                if step < 3 or turn == 0:
-                    begin(onward(way, step, half))
-                begin(across(8 - step if way == 0 else step, half))
-        expert((8 - step, step))
-    for way in range(2):
-        onward(way, 3, way).wait_recv()
-        begin(across(4, way))
-    expert((4,))
-    second.run()
-    for half in range(2):
-        cols = slice(half * HALF, (half + 1) * HALF)
-        o_ref[:, cols] = (res[:, cols] + second.result(half)).astype(BF16)
-    for copy in sent:
+        for turn, way, part in turns():
+            onward(way, step - 1, part).wait_recv()
+            if step < 3 or turn == 0:
+                begin(onward(way, step, part))
+        if step == 1:
+            expert((0, 1, 7))
+        elif step == 2:
+            expert((2, 6))
+    for turn, way, part in turns():
+        if turn == 0:
+            onward(way, 3, part).wait_recv()
+    expert((3, 4, 5))
+    second = RingSum(own.at[1], out.at[1], came.at[1], rsem.at[1], ring)
+    second.run(lambda step: None)
+    for part in range(PARTS):
+        cols = slice(part * WIDE, (part + 1) * WIDE)
+        o_ref[:, cols] = (res[:, cols] + second.result(part)).astype(BF16)
+    for copy in sent + shared:
         copy.wait_send()
     first.drain()
     second.drain()
@@ -513,23 +523,26 @@
     args[10] = args[10].T
     args[11] = args[11].T
     slots = pltpu.VMEM((4, 2, DK, 2 * DK), BF16)
-    scratch = [pltpu.VMEM(a.shape, a.dtype) for a in args] + [
+    both = {8: (2,) + args[8].shape}
+    for i in (12, 13, 14):
+        both[i] = (2,) + args[i].shape[1:]
+    scratch = [pltpu.VMEM(both.get(i, a.shape), a.dtype) for i, a in enumerate(args)] + [
         pltpu.VMEM((2, 8, 32, D), F32),
-        pltpu.VMEM((2, 8, 32, D), BF16),
-        pltpu.VMEM((2, 8, 32, D), BF16),
-        pltpu.VMEM((2, 2, 4, 2, 32, HALF), BF16),
-        pltpu.VMEM((2, 2, 4, 2, 32, HALF), BF16),
+        pltpu.VMEM((2, 2, 4, PARTS, 32, WIDE), BF16),
+        pltpu.VMEM((2, 2, 4, PARTS, 32, WIDE), BF16),
         pltpu.VMEM((32, D), F32),
-        pltpu.VMEM((8, 2, 32, HALF + 128), BF16),
-        pltpu.VMEM((8, 2, 32, HALF), BF16),
-        pltpu.VMEM(args[3].shape, BF16),
+        pltpu.VMEM((8, PARTS, 32, WIDE), BF16),
+        pltpu.VMEM((8, 32, 128), BF16),
+        pltpu.VMEM((2, 2, 256, DV), BF16),
+        pltpu.VMEM((2, 256, DV), BF16),
         slots,
         slots,
         pltpu.SemaphoreType.DMA((15,)),
-        pltpu.SemaphoreType.DMA((2, 2, 8)),
-        pltpu.SemaphoreType.DMA((2, 2, 2, 4, 2)),
-        pltpu.SemaphoreType.DMA((2, 2, 4, 2)),
-        pltpu.SemaphoreType.DMA((2, 8, 2)),
+        pltpu.SemaphoreType.DMA((2, 4)),
+        pltpu.SemaphoreType.DMA((2, 2)),
+        pltpu.SemaphoreType.DMA((2, 8)),
+        pltpu.SemaphoreType.DMA((2, 2, 2, 4, PARTS)),
+        pltpu.SemaphoreType.DMA((2, 2, 4, PARTS)),
     ]
     return pl.pallas_call(
         kernel,

time: 91.9 us -> 88.2 us (0.960)
  Pallas kernels: 89.5 us -> 86.4 us
    pallas_call x1, Pallas kernels: 89.5 us -> 86.4 us  [per_device(): pl.pallas_call(kernel, out_shape=jax.ShapeDtypeStruct(args[0].shape, BF16...]
where the time goes in v3:
time: 88.2 us; the launch traced here: 87.9 us
  Pallas kernels  86.4 us (98%)
  local copies, waits for them, and re-layouts  1.57 us (2%)
    pallas_call x1, Pallas kernels, per_device(): pl.pallas_call(kernel, out_shape=jax.ShapeDtypeStruct(args[0].shape, BF16...  86.4 us

profile of v3, /device:TPU:8, one launch (start us, length us, event | category | flops | bytes accessed | tf_op | source)
XLA Modules:
  0.0 87.9 jit_solution(14505413565594095243)
XLA Ops:
  0.0 86.4 %layer.1 = bf16[32,2048]{1,0:T(8,128)(2,1)} custom-call(bf16[32,2048]{1,0:T(8,128)(2,1)} %refs_0_.1, bf16[512,128]{1,0:T(8,128)(2,1)} %refs_1_.1, bf16[512,128]{1,0:T(8,128)(2,1)} %refs_2_.1, bf16[512,256]{1,0:T(8,128)(2,1)} %refs_3_.1, bf16[512,256]{1,0:T(8,128)(2,1)} %refs_4_.1, f32[2,512]{1,0:T(2,128)} %refs_5_.1, f32[2,512]{1,0:T(2,128)} %refs_6_.1, ...), custom_call_target="tpu_custom_call" | custom-call | tf_op jit(solution)/shard_map/layer/pallas_call | solution.py:547
  86.4 1.6 %copy.17 = bf16[32,2048]{1,0:T(8,128)(2,1)} copy(bf16[32,2048]{1,0:T(8,128)(2,1)} %layer.1) | data formatting | bytes 262144

commit v4 on v3

--- a/solution.py
+++ b/solution.py
@@ -35,7 +35,21 @@
 def mm3(a, b, dims=NN):
     ah, al = a if isinstance(a, tuple) else split(a)
     bh, bl = b if isinstance(b, tuple) else split(b)
-    return mm(ah, bh, dims) + (mm(ah, bl, dims) + mm(al, bh, dims))
+    if dims != NN:
+        return mm(ah, bh, dims) + (mm(ah, bl, dims) + mm(al, bh, dims))
+    n = bh.shape[1]
+    left = jnp.concatenate([ah, al], axis=1)
+    if n > 128:
+        return mm(left, jnp.concatenate([bh, bh], axis=0)) + mm(ah, bl)
+    right = jnp.concatenate(
+        [
+            jnp.concatenate([bh, bl], axis=1),
+            jnp.concatenate([bh, jnp.zeros_like(bl)], axis=1),
+        ],
+        axis=0,
+    )
+    both = mm(left, right)
+    return both[:, :n] + both[:, n:]
 
 
 def mm2(a, b, dims=NN):
@@ -62,43 +76,35 @@
 
 
 class Gather4:
-    def __init__(self, slots, me, right, left, ssem, rsem):
-        before, after = lax.rem(me + 3, 4), lax.rem(me + 1, 4)
-        self.own = [
-            send_to(slots.at[me], slots.at[me], ssem.at[0], rsem.at[0], "seq", right),
-            send_to(slots.at[me], slots.at[me], ssem.at[1], rsem.at[1], "seq", left),
-        ]
-        self.arrive = [
-            send_to(slots.at[before], slots.at[before], ssem.at[0], rsem.at[0], "seq", right),
-            send_to(slots.at[after], slots.at[after], ssem.at[1], rsem.at[1], "seq", left),
-        ]
-        self.onward = [
-            send_to(
-                slots.at[before, 0], slots.at[before, 0], ssem.at[2], rsem.at[2], "seq", right
-            ),
-            send_to(slots.at[after, 1], slots.at[after, 1], ssem.at[3], rsem.at[3], "seq", left),
-        ]
-        far = lax.rem(me + 2, 4)
-        self.far = [
-            send_to(slots.at[far, 0], slots.at[far, 0], ssem.at[2], rsem.at[2], "seq", right),
-            send_to(slots.at[far, 1], slots.at[far, 1], ssem.at[3], rsem.at[3], "seq", left),
-        ]
-
-    def start(self):
-        for copy in self.own:
-            copy.start()
-
-    def forward(self):
-        for came, on in zip(self.arrive, self.onward):
-            came.wait_recv()
-            on.start()
-
-    def finish(self):
-        for copy in self.far:
-            copy.wait_recv()
+    def __init__(self, slots, me, peers, ssem, rsem):
+        self.slots, self.me, self.peers, self.ssem, self.rsem = slots, me, peers, ssem, rsem
+        self.sent = []
+
+    def copy(self, d, h, i):
+        place = lax.rem(self.me + d, 4)
+        piece = self.slots.at[place, h, pl.ds(i * 64, 64)]
+        return piece, h * 2 + i
+
+    def start(self, h):
+        for i in range(2):
+            piece, at = self.copy(0, h, i)
+            for d in (2, 1, 3):
+                copy = send_to(
+                    piece, piece, self.ssem.at[d, at], self.rsem.at[d, at], "seq", self.peers[d]
+                )
+                copy.start()
+                self.sent.append(copy)
+
+    def finish(self, h):
+        for d in (1, 3, 2):
+            for i in range(2):
+                piece, at = self.copy(4 - d, h, i)
+                send_to(
+                    piece, piece, self.ssem.at[d, at], self.rsem.at[d, at], "seq", self.peers[d]
+                ).wait_recv()
 
     def drain(self):
-        for copy in self.own + self.onward:
+        for copy in self.sent:
             copy.wait_send()
 
 
@@ -109,9 +115,9 @@
     return joined + jnp.concatenate([jnp.zeros((DK, DK), F32), later[:, DK:]], axis=1)
 
 
-def seq_part(q_ref, k_ref, v_ref, g_ref, ld_ref, wr_ref, gain_ref, mix, xs, ys, sems, at, late, ready):
+def seq_part(q_ref, k_ref, v_ref, g_ref, ld_ref, wr_ref, gain_ref, mix, xs, ys, sems, at, meet, late, ready):
     xsend, xrecv, ysend, yrecv = sems
-    x, y, x_right, x_left, y_right, y_left = at
+    x, y, x_peers, y_peers = at
     chunks = q_ref.shape[0] // CH
     row = lax.broadcasted_iota(jnp.int32, (CH, CH), 0)
     col = lax.broadcasted_iota(jnp.int32, (CH, CH), 1)
@@ -125,13 +131,9 @@
         rows = slice(n * CH, (n + 1) * CH)
         k = k_ref[rows, :].astype(F32)
         k = k * lax.rsqrt(jnp.sum(k * k, axis=-1, keepdims=True) + EPS)
-        q = q_ref[rows, :].astype(F32)
-        q = q * lax.rsqrt(jnp.sum(q * q, axis=-1, keepdims=True) + EPS) * DK ** (-0.5)
         ks = split(k)
         keys.append(k)
-        queries.append(q)
         kk.append(mm3(ks, ks, NT))
-        qk.append(mm3(split(q), ks, NT))
 
     decay, grow, tail, end, strict_part, rate = {}, {}, {}, {}, {}, {}
     for n, h in pairs:
@@ -176,20 +178,28 @@
             [jnp.where(eye, end[n, h], 0.0) - fed[:, :DK], fed[:, DK:]], axis=1
         )
 
+    along_x = Gather4(xs, x, x_peers, xsend, xrecv)
+    along_y = Gather4(ys, y, y_peers, ysend, yrecv)
     prefixes = {}
     for h in range(2):
         first = compose(step[1, h], step[0, h])
         second = compose(step[3, h], step[2, h])
         whole = compose(second, first)
         xs[x, h] = whole.astype(BF16)
+        if h == 0:
+            meet()
+        along_x.start(h)
         prefixes[1, h] = step[0, h]
         prefixes[2, h] = first
         prefixes[3, h] = (step[2, h], first)
-
-    along_x = Gather4(xs, x, x_right, x_left, xsend, xrecv)
-    along_x.start()
+    late()
 
     base, mapped = {}, {}
+    for n in range(chunks):
+        q = q_ref[n * CH : (n + 1) * CH, :].astype(F32)
+        q = q * lax.rsqrt(jnp.sum(q * q, axis=-1, keepdims=True) + EPS) * DK ** (-0.5)
+        queries.append(q)
+        qk.append(mm3(split(q), split(keys[n]), NT))
     for n, h in pairs:
         scores = qk[n] * decay[n, h]
         seen = mm3(split(scores), solved[n, h])
@@ -203,14 +213,12 @@
             through = mm3(effective, ahead)
             base[n, h], mapped[n, h] = seen[:, DK:] + through[:, DK:], through[:, :DK]
 
-    along_x.forward()
-    along_x.finish()
-    along_y = Gather4(ys, y, y_right, y_left, ysend, yrecv)
     for h in range(2):
+        along_x.finish(h)
         lower = compose(xs[1, h], xs[0, h])
         upper = compose(xs[3, h], xs[2, h])
         ys[y, h] = compose(upper, lower).astype(BF16)
-    along_y.start()
+        along_y.start(h)
 
     state = {}
     inside = {}
@@ -225,18 +233,14 @@
         for other in range(1, 3):
             running = jnp.where(x > other, compose(xs[other, h], running), running)
         inside[h] = running
-    along_y.forward()
-    along_y.finish()
+    gain = gain_ref[...]
     for h in range(2):
+        along_y.finish(h)
         running = jnp.where(y > 0, ys[0, h, :, DK:].astype(F32), 0.0)
         for other in range(1, 3):
             after = mm2(ys[other, h, :, :DK], running) + ys[other, h, :, DK:].astype(F32)
             running = jnp.where(y > other, after, running)
         state[h] = split(mm3(inside[h][:, :DK], running) + inside[h][:, DK:])
-
-    late()
-    gain = gain_ref[...]
-    for h in range(2):
         cols = slice(h * DV, (h + 1) * DV)
         for n in range(chunks):
             rows = slice(n * CH, (n + 1) * CH)
@@ -271,12 +275,16 @@
             self.ring[way],
         )
 
+    def launch(self, way, part):
+        self.out[way, 0, part] = self.own[4, :, part * WIDE : (part + 1) * WIDE].astype(BF16)
+        copy = self.hop(way, 0, part)
+        copy.start()
+        self.sent.append(copy)
+
     def run(self, prepare):
-        for step in range(4):
+        for step in range(1, 4):
             prepare(step)
             for turn, way, part in turns():
-                if step == 0 and turn == 1:
-                    continue
                 d = 4 - step if way == 0 else 4 + step
                 total = self.own[d, :, part * WIDE : (part + 1) * WIDE]
                 if step >= 2 or (step == 1 and turn == 0):
@@ -325,16 +333,12 @@
     ring = (chips[1], chips[7])
     turn_at = lax.axis_index("seq")
     x, y = lax.rem(turn_at, 4), lax.div(turn_at, 4)
-    at = (
-        x,
-        y,
-        y * 4 + lax.rem(x + 1, 4),
-        y * 4 + lax.rem(x + 3, 4),
-        lax.rem(y + 1, 4) * 4 + x,
-        lax.rem(y + 3, 4) * 4 + x,
-    )
+    x_peers = [y * 4 + lax.rem(x + d, 4) for d in range(4)]
+    y_peers = [lax.rem(y + d, 4) * 4 + x for d in range(4)]
+    at = (x, y, x_peers, y_peers)
     meet = greet(
-        [("seq", peer) for peer in at[2:]] + [("exp", peer) for peer in chips[1:] + [sibling]]
+        [("seq", peer) for peer in x_peers[1:] + y_peers[1:]]
+        + [("exp", peer) for peer in chips[1:] + [sibling]]
     )
 
     loads, shared = [], []
@@ -356,13 +360,10 @@
     early, middle = (2, 1, 5, 6, 3), (10, 11, 4, 7, 0, 9)
     for i in early + middle:
         loads[i].start()
-    meet()
     for i in early:
         loads[i].wait()
     for i in weights:
         loads[i].start()
-    for copy in shared:
-        copy.start()
 
     lane = lax.broadcasted_iota(jnp.int32, (32, 128), 1).astype(F32)
     sent = []
@@ -372,6 +373,8 @@
         sent.append(copy)
 
     def late():
+        for copy in shared:
+            copy.start()
         for i in middle:
             loads[i].wait()
         ids = ids_ref[...].astype(F32)
@@ -413,6 +416,7 @@
         ys,
         seq_sems,
         at,
+        meet,
         late,
         lambda h: begin(mix_copy(h)),
     )
@@ -435,6 +439,10 @@
             own[0, d] = block[32 * i : 32 * i + 32]
 
     first = RingSum(own.at[0], out.at[0], came.at[0], rsem.at[0], ring)
+    project((4,))
+    for turn, way, part in turns():
+        if turn == 0:
+            first.launch(way, part)
     first.run(lambda step: project(((4,), (3, 5), (2, 6), (1, 7), (0,))[step]))
     for part in range(PARTS):
         cols = slice(part * WIDE, (part + 1) * WIDE)
@@ -474,16 +482,30 @@
                 share_table(8 - d).wait_recv()
         shares = jnp.concatenate([table[d] for d in offsets], axis=0).astype(F32)
         lanes = lax.broadcasted_iota(jnp.int32, shares.shape, 1)
-        total = None
+        hidden, share = [], []
         for e in range(2):
             gate = mm(picked, gw[e])
             up = mm(picked, uw[e])
-            hidden = (gate / (1.0 + jnp.exp(-gate)) * up).astype(BF16)
-            produced = mm(hidden, dw[e]).astype(BF16).astype(F32)
-            share = jnp.sum(jnp.where(lanes == z * 2 + e, shares, 0.0), axis=1, keepdims=True)
-            total = produced * share if total is None else total + produced * share
-        for i, d in enumerate(offsets):
-            own[1, d] = total[32 * i : 32 * i + 32]
+            hidden.append((gate / (1.0 + jnp.exp(-gate)) * up).astype(BF16))
+            share.append(
+                jnp.sum(jnp.where(lanes == z * 2 + e, shares, 0.0), axis=1, keepdims=True)
+            )
+
+        def down(part):
+            cols = slice(part * WIDE, (part + 1) * WIDE)
+            total = sum(
+                mm(hidden[e], dw[e, :, cols]).astype(BF16).astype(F32) * share[e]
+                for e in range(2)
+            )
+            for i, d in enumerate(offsets):
+                own[1, d, :, cols] = total[32 * i : 32 * i + 32]
+
+        return down
+
+    def expert_all(offsets):
+        down = expert(offsets)
+        for part in range(PARTS):
+            down(part)
 
     for turn, way, part in turns():
         begin(onward(way, 0, part))
@@ -497,14 +519,18 @@
             if step < 3 or turn == 0:
                 begin(onward(way, step, part))
         if step == 1:
-            expert((0, 1, 7))
+            expert_all((0, 1, 7))
         elif step == 2:
-            expert((2, 6))
+            expert_all((2, 6))
     for turn, way, part in turns():
         if turn == 0:
             onward(way, 3, part).wait_recv()
-    expert((3, 4, 5))
     second = RingSum(own.at[1], out.at[1], came.at[1], rsem.at[1], ring)
+    down = expert((3, 4, 5))
+    for turn, way, part in turns():
+        if turn == 0:
+            down(part)
+            second.launch(way, part)
     second.run(lambda step: None)
     for part in range(PARTS):
         cols = slice(part * WIDE, (part + 1) * WIDE)
@@ -549,7 +575,7 @@
         out_shape=jax.ShapeDtypeStruct(args[0].shape, BF16),
         in_specs=[pl.BlockSpec(memory_space=pl.ANY)] * 15,
         out_specs=pl.BlockSpec(memory_space=pltpu.VMEM),
-        scratch_shapes=scratch + [pltpu.SemaphoreType.DMA((4,))] * 4,
+        scratch_shapes=scratch + [pltpu.SemaphoreType.DMA((4, 4))] * 4,
         compiler_params=pltpu.CompilerParams(
             collective_id=0, has_side_effects=True, vmem_limit_bytes=62 * 1024 * 1024
         ),

time: 88.2 us -> 80.5 us (0.913)
  Pallas kernels: 86.4 us -> 78.8 us
    pallas_call x1, Pallas kernels: 86.4 us -> 78.8 us  [per_device(): pl.pallas_call(kernel, out_shape=jax.ShapeDtypeStruct(args[0].shape, BF16...]
where the time goes in v4:
time: 80.5 us; the launch traced here: 80.4 us
  Pallas kernels  78.8 us (98%)
  local copies, waits for them, and re-layouts  1.57 us (2%)
    pallas_call x1, Pallas kernels, per_device(): pl.pallas_call(kernel, out_shape=jax.ShapeDtypeStruct(args[0].shape, BF16...  78.8 us

profile of v4, /device:TPU:8, one launch (start us, length us, event | category | flops | bytes accessed | tf_op | source)
XLA Modules:
  0.0 80.4 jit_solution(9050421387137116384)
XLA Ops:
  0.0 78.8 %layer.1 = bf16[32,2048]{1,0:T(8,128)(2,1)} custom-call(bf16[32,2048]{1,0:T(8,128)(2,1)} %refs_0_.1, bf16[512,128]{1,0:T(8,128)(2,1)} %refs_1_.1, bf16[512,128]{1,0:T(8,128)(2,1)} %refs_2_.1, bf16[512,256]{1,0:T(8,128)(2,1)} %refs_3_.1, bf16[512,256]{1,0:T(8,128)(2,1)} %refs_4_.1, f32[2,512]{1,0:T(2,128)} %refs_5_.1, f32[2,512]{1,0:T(2,128)} %refs_6_.1, ...), custom_call_target="tpu_custom_call" | custom-call | tf_op jit(solution)/shard_map/layer/pallas_call | solution.py:573
  78.8 1.6 %copy.17 = bf16[32,2048]{1,0:T(8,128)(2,1)} copy(bf16[32,2048]{1,0:T(8,128)(2,1)} %layer.1) | data formatting | bytes 262144

commit v5 on v4

--- a/solution.py
+++ b/solution.py
@@ -115,7 +115,7 @@
     return joined + jnp.concatenate([jnp.zeros((DK, DK), F32), later[:, DK:]], axis=1)
 
 
-def seq_part(q_ref, k_ref, v_ref, g_ref, ld_ref, wr_ref, gain_ref, mix, xs, ys, sems, at, meet, late, ready):
+def seq_part(q_ref, k_ref, v_ref, g_ref, ld_ref, wr_ref, gain_ref, mix, xs, ys, sems, at, need, meet, late, ready):
     xsend, xrecv, ysend, yrecv = sems
     x, y, x_peers, y_peers = at
     chunks = q_ref.shape[0] // CH
@@ -127,6 +127,7 @@
     pairs = [(n, h) for n in range(chunks) for h in range(2)]
 
     keys, kk, qk, queries = [], [], [], []
+    need(2)
     for n in range(chunks):
         rows = slice(n * CH, (n + 1) * CH)
         k = k_ref[rows, :].astype(F32)
@@ -136,52 +137,54 @@
         kk.append(mm3(ks, ks, NT))
 
     decay, grow, tail, end, strict_part, rate = {}, {}, {}, {}, {}, {}
-    for n, h in pairs:
-        ld_row = ld_ref[h : h + 1, n * CH : (n + 1) * CH]
-        ld_all = jnp.broadcast_to(ld_row, (CH, CH))
-        wr_all = jnp.broadcast_to(wr_ref[h : h + 1, n * CH : (n + 1) * CH], (CH, CH))
-        ld_col = jnp.sum(jnp.where(eye, ld_all, 0.0), axis=1, keepdims=True)
-        cum_col = jnp.sum(jnp.where(causal, ld_all, 0.0), axis=1, keepdims=True)
-        cum_row = jnp.sum(jnp.where(row <= col, ld_col, 0.0), axis=0, keepdims=True)
-        rate[n, h] = jnp.sum(jnp.where(eye, wr_all, 0.0), axis=1, keepdims=True)
-        total = jnp.sum(ld_row, axis=1, keepdims=True)
-        decay[n, h] = jnp.where(causal, jnp.exp(jnp.where(causal, cum_col - cum_row, 0.0)), 0.0)
-        grow[n, h] = jnp.exp(cum_col)
-        tail[n, h] = jnp.exp(total - cum_col)
-        end[n, h] = jnp.exp(total)
-        strict_part[n, h] = jnp.where(strict, kk[n] * decay[n, h] * rate[n, h], 0.0)
-
-    inverse = {}
-    for p in pairs:
-        low = jnp.where((row // 2 == col // 2) & strict, strict_part[p], 0.0)
-        inverse[p] = jnp.where(eye, 1.0, -low)
-    width = 2
-    while width < CH:
-        mask = (row // (2 * width) == col // (2 * width)) & (row // width > col // width)
-        inner = {}
-        held = {}
-        for p in pairs:
-            held[p] = split(inverse[p])
-            inner[p] = mm3(split(jnp.where(mask, strict_part[p], 0.0)), held[p])
-        for p in pairs:
-            inverse[p] = inverse[p] - mm3(held[p], split(inner[p]))
-        width *= 2
-
-    step, solved = {}, {}
-    for n, h in pairs:
-        value = v_ref[n * CH : (n + 1) * CH, h * DV : (h + 1) * DV].astype(F32)
-        sides = jnp.concatenate([keys[n] * (rate[n, h] * grow[n, h]), value * rate[n, h]], axis=1)
-        solved[n, h] = split(mm3(inverse[n, h], sides))
-    for n, h in pairs:
-        fed = mm3(split(keys[n] * tail[n, h]), solved[n, h], TN)
-        step[n, h] = jnp.concatenate(
-            [jnp.where(eye, end[n, h], 0.0) - fed[:, :DK], fed[:, DK:]], axis=1
-        )
-
+    step, solved, prefixes = {}, {}, {}
     along_x = Gather4(xs, x, x_peers, xsend, xrecv)
     along_y = Gather4(ys, y, y_peers, ysend, yrecv)
-    prefixes = {}
+    need(5, 6)
     for h in range(2):
+        mine = [(n, h) for n in range(chunks)]
+        for n, h in mine:
+            ld_row = ld_ref[h : h + 1, n * CH : (n + 1) * CH]
+            ld_all = jnp.broadcast_to(ld_row, (CH, CH))
+            wr_all = jnp.broadcast_to(wr_ref[h : h + 1, n * CH : (n + 1) * CH], (CH, CH))
+            ld_col = jnp.sum(jnp.where(eye, ld_all, 0.0), axis=1, keepdims=True)
+            cum_col = jnp.sum(jnp.where(causal, ld_all, 0.0), axis=1, keepdims=True)
+            cum_row = jnp.sum(jnp.where(row <= col, ld_col, 0.0), axis=0, keepdims=True)
+            rate[n, h] = jnp.sum(jnp.where(eye, wr_all, 0.0), axis=1, keepdims=True)
+            total = jnp.sum(ld_row, axis=1, keepdims=True)
+            decay[n, h] = jnp.where(causal, jnp.exp(jnp.where(causal, cum_col - cum_row, 0.0)), 0.0)
+            grow[n, h] = jnp.exp(cum_col)
+            tail[n, h] = jnp.exp(total - cum_col)
+            end[n, h] = jnp.exp(total)
+            strict_part[n, h] = jnp.where(strict, kk[n] * decay[n, h] * rate[n, h], 0.0)
+
+        inverse = {}
+        for p in mine:
+            low = jnp.where((row // 2 == col // 2) & strict, strict_part[p], 0.0)
+            inverse[p] = jnp.where(eye, 1.0, -low)
+        width = 2
+        while width < CH:
+            mask = (row // (2 * width) == col // (2 * width)) & (row // width > col // width)
+            inner = {}
+            held = {}
+            for p in mine:
+                held[p] = split(inverse[p])
+                inner[p] = mm3(split(jnp.where(mask, strict_part[p], 0.0)), held[p])
+            for p in mine:
+                inverse[p] = inverse[p] - mm3(held[p], split(inner[p]))
+            width *= 2
+
+        if h == 0:
+            need(3)
+        for n, h in mine:
+            value = v_ref[n * CH : (n + 1) * CH, h * DV : (h + 1) * DV].astype(F32)
+            sides = jnp.concatenate([keys[n] * (rate[n, h] * grow[n, h]), value * rate[n, h]], axis=1)
+            solved[n, h] = split(mm3(inverse[n, h], sides))
+        for n, h in mine:
+            fed = mm3(split(keys[n] * tail[n, h]), solved[n, h], TN)
+            step[n, h] = jnp.concatenate(
+                [jnp.where(eye, end[n, h], 0.0) - fed[:, :DK], fed[:, DK:]], axis=1
+            )
         first = compose(step[1, h], step[0, h])
         second = compose(step[3, h], step[2, h])
         whole = compose(second, first)
@@ -195,6 +198,7 @@
     late()
 
     base, mapped = {}, {}
+    need(1)
     for n in range(chunks):
         q = q_ref[n * CH : (n + 1) * CH, :].astype(F32)
         q = q * lax.rsqrt(jnp.sum(q * q, axis=-1, keepdims=True) + EPS) * DK ** (-0.5)
@@ -284,7 +288,7 @@
     def run(self, prepare):
         for step in range(1, 4):
             prepare(step)
-            for turn, way, part in turns():
+            for turn, way, part in turns()[2 * (PARTS // 2) :] + turns()[: 2 * (PARTS // 2)]:
                 d = 4 - step if way == 0 else 4 + step
                 total = self.own[d, :, part * WIDE : (part + 1) * WIDE]
                 if step >= 2 or (step == 1 and turn == 0):
@@ -321,8 +325,8 @@
 def kernel(*refs):
     inputs, o_ref, scratch = refs[:15], refs[15], refs[16:]
     held, scratch = scratch[:15], scratch[15:]
-    (own, out, came, res, tokens, table, mix, mix_in, xs, ys) = scratch[:10]
-    (wsem, csem, msem, tsem, rsem, gsem, *seq_sems) = scratch[10:]
+    (own, out, came, res, tokens, normed, table, mix, mix_in, xs, ys) = scratch[:11]
+    (wsem, csem, msem, tsem, rsem, gsem, *seq_sems) = scratch[11:]
     (hid_ref, q, k, v, g, ld, wr, gain, ow, post_ref, ids_ref, route_ref, gw, uw, dw) = held
     weights = (8, 12, 13, 14)
 
@@ -357,13 +361,13 @@
         )
         for n, i in enumerate(weights)
     ]
-    early, middle = (2, 1, 5, 6, 3), (10, 11, 4, 7, 0, 9)
+    early, middle = (2, 5, 6, 3, 1), (10, 11, 4, 7, 0, 9)
     for i in early + middle:
         loads[i].start()
-    for i in early:
-        loads[i].wait()
-    for i in weights:
-        loads[i].start()
+
+    def need(*which):
+        for i in which:
+            loads[i].wait()
 
     lane = lax.broadcasted_iota(jnp.int32, (32, 128), 1).astype(F32)
     sent = []
@@ -373,7 +377,8 @@
         sent.append(copy)
 
     def late():
-        for copy in shared:
+        for i, copy in zip(weights, shared):
+            loads[i].start()
             copy.start()
         for i in middle:
             loads[i].wait()
@@ -416,47 +421,36 @@
         ys,
         seq_sems,
         at,
+        need,
         meet,
         late,
         lambda h: begin(mix_copy(h)),
     )
 
+    def mixed_rows(ref, offsets):
+        rows = [pl.ds(pl.multiple_of(lax.rem(z + d, 8) * 32, 32), 32) for d in offsets]
+        return jnp.concatenate(
+            [jnp.concatenate([ref[h, r] for h in range(2)], axis=1) for r in rows], axis=0
+        )
+
+    def project(offsets):
+        block = mm(mixed_rows(mix_in, offsets), ow[1 - core])
+        for i, d in enumerate(offsets):
+            own[0, d] = own[0, d] + block[32 * i : 32 * i + 32]
+
     loads[8].wait()
+    block = mm(mixed_rows(mix.at[core], range(8)), ow[core])
+    for d in range(8):
+        own[0, d] = block[32 * d : 32 * d + 32]
     arriving[0].wait_recv()
     for h in range(2):
         mix_copy(h).wait_recv()
-
-    def project(offsets):
-        rows = [pl.ds(pl.multiple_of(lax.rem(z + d, 8) * 32, 32), 32) for d in offsets]
-        mine, other = (
-            jnp.concatenate(
-                [jnp.concatenate([ref[h, r] for h in range(2)], axis=1) for r in rows], axis=0
-            )
-            for ref in (mix.at[core], mix_in)
-        )
-        block = mm(mine, ow[core]) + mm(other, ow[1 - core])
-        for i, d in enumerate(offsets):
-            own[0, d] = block[32 * i : 32 * i + 32]
-
     first = RingSum(own.at[0], out.at[0], came.at[0], rsem.at[0], ring)
     project((4,))
     for turn, way, part in turns():
         if turn == 0:
             first.launch(way, part)
     first.run(lambda step: project(((4,), (3, 5), (2, 6), (1, 7), (0,))[step]))
-    for part in range(PARTS):
-        cols = slice(part * WIDE, (part + 1) * WIDE)
-        res[:, cols] = hid_ref[:, cols].astype(F32) + first.result(part)
-
-    residual = res[...]
-    normed = (
-        residual
-        * lax.rsqrt(jnp.mean(residual * residual, axis=-1, keepdims=True) + EPS)
-        * post_ref[...]
-    ).astype(BF16)
-    for part in range(PARTS):
-        tokens[0, part] = normed[:, part * WIDE : (part + 1) * WIDE]
-
     def onward(way, step, part):
         src = (8 - step) % 8 if way == 0 else step
         dst = 7 - step if way == 0 else step + 1
@@ -469,27 +463,47 @@
             ring[way],
         )
 
+    def settle(offsets):
+        for d in offsets:
+            row = jnp.concatenate([tokens[d, part] for part in range(PARTS)], axis=1).astype(F32)
+            scale = lax.rsqrt(jnp.mean(row * row, axis=-1, keepdims=True) + EPS)
+            normed[d] = (row * scale * post_ref[...]).astype(BF16)
+
     def expert(offsets):
-        picked = jnp.concatenate(
-            [
-                jnp.concatenate([tokens[d, part] for part in range(PARTS)], axis=1)
-                for d in offsets
-            ],
-            axis=0,
-        )
         for d in offsets:
             if d > 0:
                 share_table(8 - d).wait_recv()
         shares = jnp.concatenate([table[d] for d in offsets], axis=0).astype(F32)
         lanes = lax.broadcasted_iota(jnp.int32, shares.shape, 1)
         hidden, share = [], []
-        for e in range(2):
-            gate = mm(picked, gw[e])
-            up = mm(picked, uw[e])
+
+        def close(e, gate, up):
             hidden.append((gate / (1.0 + jnp.exp(-gate)) * up).astype(BF16))
             share.append(
                 jnp.sum(jnp.where(lanes == z * 2 + e, shares, 0.0), axis=1, keepdims=True)
             )
+
+        def widen(e):
+            picked = jnp.concatenate([normed[d] for d in offsets], axis=0)
+            close(e, mm(picked, gw[e]), mm(picked, uw[e]))
+
+        def widen_late():
+            sums = [[0.0, 0.0], [0.0, 0.0]]
+            square = 0.0
+            for i in range(PARTS // 2):
+                for way in range(2):
+                    onward(way, 3, way * (PARTS // 2) + i).wait_recv()
+                for part in (i, PARTS // 2 + i):
+                    cols = slice(part * WIDE, (part + 1) * WIDE)
+                    row = jnp.concatenate([tokens[d, part] for d in offsets], axis=0).astype(F32)
+                    square = square + jnp.sum(row * row, axis=-1, keepdims=True)
+                    row = (row * post_ref[:, cols]).astype(BF16)
+                    for e in range(2):
+                        for k, w in enumerate((gw, uw)):
+                            sums[e][k] = sums[e][k] + mm(row, w[e, cols, :])
+            scale = lax.rsqrt(square * (1.0 / D) + EPS)
+            for e in range(2):
+                close(e, sums[e][0] * scale, sums[e][1] * scale)
 
         def down(part):
             cols = slice(part * WIDE, (part + 1) * WIDE)
@@ -500,39 +514,52 @@
             for i, d in enumerate(offsets):
                 own[1, d, :, cols] = total[32 * i : 32 * i + 32]
 
-        return down
-
-    def expert_all(offsets):
-        down = expert(offsets)
-        for part in range(PARTS):
-            down(part)
-
-    for turn, way, part in turns():
-        begin(onward(way, 0, part))
+        return widen, widen_late, down
+
+    for part in (i + j for i in range(PARTS // 2) for j in (0, PARTS // 2)):
+        cols = slice(part * WIDE, (part + 1) * WIDE)
+        block = hid_ref[:, cols].astype(F32) + first.result(part)
+        res[:, cols] = block
+        tokens[0, part] = block.astype(BF16)
+        ahead = 0 if part < PARTS // 2 else 1
+        for way in (ahead, 1 - ahead):
+            begin(onward(way, 0, part))
+    settle((0,))
     for i in weights[1:]:
         loads[i].wait()
     for copy in arriving[1:]:
         copy.wait_recv()
-    for step in range(1, 4):
+
+    def pass_on(step):
         for turn, way, part in turns():
             onward(way, step - 1, part).wait_recv()
             if step < 3 or turn == 0:
                 begin(onward(way, step, part))
-        if step == 1:
-            expert_all((0, 1, 7))
-        elif step == 2:
-            expert_all((2, 6))
-    for turn, way, part in turns():
-        if turn == 0:
-            onward(way, 3, part).wait_recv()
+        if step < 3:
+            settle((8 - step, step))
+
+    pass_on(1)
+    near_widen, _, near_down = expert((0, 1, 7))
+    near_widen(0)
+    near_widen(1)
+    pass_on(2)
+    for part in range(PARTS):
+        near_down(part)
+    next_widen, _, next_down = expert((2, 6))
+    next_widen(0)
+    pass_on(3)
+    next_widen(1)
+    for part in range(PARTS):
+        next_down(part)
     second = RingSum(own.at[1], out.at[1], came.at[1], rsem.at[1], ring)
-    down = expert((3, 4, 5))
+    _, widen_late, down = expert((3, 4, 5))
+    widen_late()
     for turn, way, part in turns():
         if turn == 0:
             down(part)
             second.launch(way, part)
     second.run(lambda step: None)
-    for part in range(PARTS):
+    for part in (i + j for i in range(PARTS // 2) for j in (0, PARTS // 2)):
         cols = slice(part * WIDE, (part + 1) * WIDE)
         o_ref[:, cols] = (res[:, cols] + second.result(part)).astype(BF16)
     for copy in sent + shared:
@@ -558,6 +585,7 @@
         pltpu.VMEM((2, 2, 4, PARTS, 32, WIDE), BF16),
         pltpu.VMEM((32, D), F32),
         pltpu.VMEM((8, PARTS, 32, WIDE), BF16),
+        pltpu.VMEM((8, 32, D), BF16),
         pltpu.VMEM((8, 32, 128), BF16),
         pltpu.VMEM((2, 2, 256, DV), BF16),
         pltpu.VMEM((2, 256, DV), BF16),

time: 80.5 us -> 74.6 us (0.927)
  Pallas kernels: 78.8 us -> 72.4 us
    pallas_call x1, Pallas kernels: 78.8 us -> 72.4 us  [per_device(): pl.pallas_call(kernel, out_shape=jax.ShapeDtypeStruct(args[0].shape, BF16...]
where the time goes in v5:
time: 74.6 us; the launch traced here: 74 us
  Pallas kernels  72.4 us (97%)
  local copies, waits for them, and re-layouts  1.57 us (2%)
    pallas_call x1, Pallas kernels, per_device(): pl.pallas_call(kernel, out_shape=jax.ShapeDtypeStruct(args[0].shape, BF16...  72.4 us
    unnamed x1, local copies, waits for them, and re-layouts  1.57 us

profile of v5, /device:TPU:8, one launch (start us, length us, event | category | flops | bytes accessed | tf_op | source)
XLA Modules:
  0.0 74.0 jit_solution(6983856800369753048)
XLA Ops:
  0.0 72.4 %layer.1 = bf16[32,2048]{1,0:T(8,128)(2,1)} custom-call(bf16[32,2048]{1,0:T(8,128)(2,1)} %refs_0_.1, bf16[512,128]{1,0:T(8,128)(2,1)} %refs_1_.1, bf16[512,128]{1,0:T(8,128)(2,1)} %refs_2_.1, bf16[512,256]{1,0:T(8,128)(2,1)} %refs_3_.1, bf16[512,256]{1,0:T(8,128)(2,1)} %refs_4_.1, f32[2,512]{1,0:T(2,128)} %refs_5_.1, f32[2,512]{1,0:T(2,128)} %refs_6_.1, ...), custom_call_target="tpu_custom_call" | custom-call | tf_op jit(solution)/shard_map/layer/pallas_call | solution.py:601
  72.5 1.6 %copy.17 = bf16[32,2048]{1,0:T(8,128)(2,1)} copy(bf16[32,2048]{1,0:T(8,128)(2,1)} %layer.1) | data formatting | bytes 262144

commit v6 on v5

--- a/solution.py
+++ b/solution.py
@@ -76,8 +76,9 @@
 
 
 class Gather4:
-    def __init__(self, slots, me, peers, ssem, rsem):
+    def __init__(self, slots, me, peers, ssem, rsem, upward=False):
         self.slots, self.me, self.peers, self.ssem, self.rsem = slots, me, peers, ssem, rsem
+        self.upward = upward
         self.sent = []
 
     def copy(self, d, h, i):
@@ -92,20 +93,27 @@
                 copy = send_to(
                     piece, piece, self.ssem.at[d, at], self.rsem.at[d, at], "seq", self.peers[d]
                 )
-                copy.start()
-                self.sent.append(copy)
+                self.when(self.me + d < 4, copy.start)
+                self.sent.append((d, copy))
+
+    def when(self, holds, act):
+        if self.upward:
+            pl.when(holds)(act)
+        else:
+            act()
 
     def finish(self, h):
         for d in (1, 3, 2):
             for i in range(2):
                 piece, at = self.copy(4 - d, h, i)
-                send_to(
+                came = send_to(
                     piece, piece, self.ssem.at[d, at], self.rsem.at[d, at], "seq", self.peers[d]
-                ).wait_recv()
+                )
+                self.when(self.me >= d, came.wait_recv)
 
     def drain(self):
-        for copy in self.sent:
-            copy.wait_send()
+        for d, copy in self.sent:
+            self.when(self.me + d < 4, copy.wait_send)
 
 
 def compose(later, earlier):
@@ -139,7 +147,7 @@
     decay, grow, tail, end, strict_part, rate = {}, {}, {}, {}, {}, {}
     step, solved, prefixes = {}, {}, {}
     along_x = Gather4(xs, x, x_peers, xsend, xrecv)
-    along_y = Gather4(ys, y, y_peers, ysend, yrecv)
+    along_y = Gather4(ys, y, y_peers, ysend, yrecv, upward=True)
     need(5, 6)
     for h in range(2):
         mine = [(n, h) for n in range(chunks)]
@@ -340,6 +348,7 @@
     x_peers = [y * 4 + lax.rem(x + d, 4) for d in range(4)]
     y_peers = [lax.rem(y + d, 4) * 4 + x for d in range(4)]
     at = (x, y, x_peers, y_peers)
+    ys[...] = jnp.zeros_like(ys)
     meet = greet(
         [("seq", peer) for peer in x_peers[1:] + y_peers[1:]]
         + [("exp", peer) for peer in chips[1:] + [sibling]]

time: 74.6 us -> 73.2 us (0.981)
  Pallas kernels: 72.4 us -> 71 us
    pallas_call x1, Pallas kernels: 72.4 us -> 71 us  [per_device(): pl.pallas_call(kernel, out_shape=jax.ShapeDtypeStruct(args[0].shape, BF16...]
where the time goes in v6:
time: 73.2 us; the launch traced here: 72.6 us
  Pallas kernels  71 us (97%)
  local copies, waits for them, and re-layouts  1.57 us (2%)
    pallas_call x1, Pallas kernels, per_device(): pl.pallas_call(kernel, out_shape=jax.ShapeDtypeStruct(args[0].shape, BF16...  71 us
    unnamed x1, local copies, waits for them, and re-layouts  1.57 us

profile of v6, /device:TPU:8, one launch (start us, length us, event | category | flops | bytes accessed | tf_op | source)
XLA Modules:
  0.0 72.6 jit_solution(17444563007380579302)
XLA Ops:
  0.0 71.0 %layer.1 = bf16[32,2048]{1,0:T(8,128)(2,1)} custom-call(bf16[32,2048]{1,0:T(8,128)(2,1)} %refs_0_.1, bf16[512,128]{1,0:T(8,128)(2,1)} %refs_1_.1, bf16[512,128]{1,0:T(8,128)(2,1)} %refs_2_.1, bf16[512,256]{1,0:T(8,128)(2,1)} %refs_3_.1, bf16[512,256]{1,0:T(8,128)(2,1)} %refs_4_.1, f32[2,512]{1,0:T(2,128)} %refs_5_.1, f32[2,512]{1,0:T(2,128)} %refs_6_.1, ...), custom_call_target="tpu_custom_call" | custom-call | tf_op jit(solution)/shard_map/layer/pallas_call | solution.py:610
  71.0 1.6 %copy.17 = bf16[32,2048]{1,0:T(8,128)(2,1)} copy(bf16[32,2048]{1,0:T(8,128)(2,1)} %layer.1) | data formatting | bytes 262144

commit v7 on v6

--- a/solution.py
+++ b/solution.py
@@ -172,15 +172,17 @@
             inverse[p] = jnp.where(eye, 1.0, -low)
         width = 2
         while width < CH:
-            mask = (row // (2 * width) == col // (2 * width)) & (row // width > col // width)
-            inner = {}
-            held = {}
+            mask = (row // (4 * width) == col // (4 * width)) & (row // width > col // width)
+            held, lower, rest, twice = {}, {}, {}, {}
             for p in mine:
                 held[p] = split(inverse[p])
-                inner[p] = mm3(split(jnp.where(mask, strict_part[p], 0.0)), held[p])
+                lower[p] = split(mm3(held[p], split(jnp.where(mask, strict_part[p], 0.0))))
             for p in mine:
-                inverse[p] = inverse[p] - mm3(held[p], split(inner[p]))
-            width *= 2
+                rest[p] = inverse[p] - mm3(lower[p], held[p])
+                twice[p] = split(mm3(lower[p], lower[p]))
+            for p in mine:
+                inverse[p] = rest[p] + mm3(twice[p], split(rest[p]))
+            width *= 4
 
         if h == 0:
             need(3)

time: 73.2 us -> 72.1 us (0.985)
  no operation moved by 1% of the time
where the time goes in v7:
time: 72.1 us; the launch traced here: 72 us
  Pallas kernels  70.4 us (98%)
  local copies, waits for them, and re-layouts  1.57 us (2%)
    pallas_call x1, Pallas kernels, per_device(): pl.pallas_call(kernel, out_shape=jax.ShapeDtypeStruct(args[0].shape, BF16...  70.4 us
    unnamed x1, local copies, waits for them, and re-layouts  1.57 us

profile of v7, /device:TPU:8, one launch (start us, length us, event | category | flops | bytes accessed | tf_op | source)
XLA Modules:
  0.0 72.0 jit_solution(8681977115000514470)
XLA Ops:
  0.0 70.4 %layer.1 = bf16[32,2048]{1,0:T(8,128)(2,1)} custom-call(bf16[32,2048]{1,0:T(8,128)(2,1)} %refs_0_.1, bf16[512,128]{1,0:T(8,128)(2,1)} %refs_1_.1, bf16[512,128]{1,0:T(8,128)(2,1)} %refs_2_.1, bf16[512,256]{1,0:T(8,128)(2,1)} %refs_3_.1, bf16[512,256]{1,0:T(8,128)(2,1)} %refs_4_.1, f32[2,512]{1,0:T(2,128)} %refs_5_.1, f32[2,512]{1,0:T(2,128)} %refs_6_.1, ...), custom_call_target="tpu_custom_call" | custom-call | tf_op jit(solution)/shard_map/layer/pallas_call | solution.py:612
  70.4 1.6 %copy.17 = bf16[32,2048]{1,0:T(8,128)(2,1)} copy(bf16[32,2048]{1,0:T(8,128)(2,1)} %layer.1) | data formatting | bytes 262144

commit v8 on v7

--- a/solution.py
+++ b/solution.py
@@ -123,7 +123,7 @@
     return joined + jnp.concatenate([jnp.zeros((DK, DK), F32), later[:, DK:]], axis=1)
 
 
-def seq_part(q_ref, k_ref, v_ref, g_ref, ld_ref, wr_ref, gain_ref, mix, xs, ys, sems, at, need, meet, late, ready):
+def seq_part(q_ref, k_ref, v_ref, g_ref, ld_ref, wr_ref, gain_ref, mix, xs, ys, sems, at, need, meet, give, late, ready):
     xsend, xrecv, ysend, yrecv = sems
     x, y, x_peers, y_peers = at
     chunks = q_ref.shape[0] // CH
@@ -202,6 +202,8 @@
         if h == 0:
             meet()
         along_x.start(h)
+        if h == 0:
+            give()
         prefixes[1, h] = step[0, h]
         prefixes[2, h] = first
         prefixes[3, h] = (step[2, h], first)
@@ -387,10 +389,12 @@
         copy.start()
         sent.append(copy)
 
-    def late():
+    def give():
         for i, copy in zip(weights, shared):
             loads[i].start()
             copy.start()
+
+    def late():
         for i in middle:
             loads[i].wait()
         ids = ids_ref[...].astype(F32)
@@ -434,6 +438,7 @@
         at,
         need,
         meet,
+        give,
         late,
         lambda h: begin(mix_copy(h)),
     )

time: 72.1 us -> 72.1 us (level)
  no operation moved by 1% of the time
where the time goes in v8:
time: 72.1 us; the launch traced here: 71.8 us
  Pallas kernels  70.3 us (98%)
  local copies, waits for them, and re-layouts  1.57 us (2%)
    pallas_call x1, Pallas kernels, per_device(): pl.pallas_call(kernel, out_shape=jax.ShapeDtypeStruct(args[0].shape, BF16...  70.3 us
    unnamed x1, local copies, waits for them, and re-layouts  1.57 us

profile of v8, /device:TPU:8, one launch (start us, length us, event | category | flops | bytes accessed | tf_op | source)
XLA Modules:
  0.0 71.8 jit_solution(6401393434440676888)
XLA Ops:
  0.0 70.3 %layer.1 = bf16[32,2048]{1,0:T(8,128)(2,1)} custom-call(bf16[32,2048]{1,0:T(8,128)(2,1)} %refs_0_.1, bf16[512,128]{1,0:T(8,128)(2,1)} %refs_1_.1, bf16[512,128]{1,0:T(8,128)(2,1)} %refs_2_.1, bf16[512,256]{1,0:T(8,128)(2,1)} %refs_3_.1, bf16[512,256]{1,0:T(8,128)(2,1)} %refs_4_.1, f32[2,512]{1,0:T(2,128)} %refs_5_.1, f32[2,512]{1,0:T(2,128)} %refs_6_.1, ...), custom_call_target="tpu_custom_call" | custom-call | tf_op jit(solution)/shard_map/layer/pallas_call | solution.py:617
  70.3 1.6 %copy.17 = bf16[32,2048]{1,0:T(8,128)(2,1)} copy(bf16[32,2048]{1,0:T(8,128)(2,1)} %layer.1) | data formatting | bytes 262144
